TPU v7x, 32 devices: a whole 2x2x4 slice. The times are simulated.
32 devices in a mesh: expert: 8 (over z, y), dp: 4 (over x, core).
Axes of the slice: x: 2, y: 2, z: 4, core: 2. Of those that a mesh axis runs over, the one named last changes fastest.
Arguments:
- tokens: bfloat16 [4096, 2048], P(('expert', 'dp')), may hold values from -6 to 6
- cotangent: bfloat16 [4096, 2048], P(('expert', 'dp')), may hold values from -3 to 3
- route_ids: int32 [4096, 2], P(('expert', 'dp')), may hold values from 0 to 8, as said below
- route_weights: float32 [4096, 2], P(('expert', 'dp')), may hold values from 0.2 to 1
- cold_gate: bfloat16 [8, 768, 2048], P('expert', 'dp'), may hold values from -0.125 to 0.125
- cold_up: bfloat16 [8, 768, 2048], P('expert', 'dp'), may hold values from -0.125 to 0.125
- cold_down: bfloat16 [8, 768, 2048], P('expert', 'dp'), may hold values from -0.21875 to 0.21875
- hot_gate: bfloat16 [1, 768, 2048], P(None, 'dp'), may hold values from -0.125 to 0.125
- hot_up: bfloat16 [1, 768, 2048], P(None, 'dp'), may hold values from -0.125 to 0.125
- hot_down: bfloat16 [1, 768, 2048], P(None, 'dp'), may hold values from -0.21875 to 0.21875
Outputs:
- mixed: bfloat16 [4096, 2048], P(('expert', 'dp'))
- token_grad: bfloat16 [4096, 2048], P(('expert', 'dp'))
- route_grad: float32 [4096, 2], P(('expert', 'dp'))
- cold_gate_grad: bfloat16 [8, 768, 2048], P('expert', 'dp')
- cold_up_grad: bfloat16 [8, 768, 2048], P('expert', 'dp')
- cold_down_grad: bfloat16 [8, 768, 2048], P('expert', 'dp')
- hot_gate_grad: float32 [1, 768, 2048], P(None, 'dp', 'expert')
- hot_up_grad: float32 [1, 768, 2048], P(None, 'dp', 'expert')
- hot_down_grad: float32 [1, 768, 2048], P(None, 'dp', 'expert')
Inputs may be any that keep to these rules, and one draw needn't show every extreme that they name: `route_ids`: each row names 2 different experts. Experts 8 and above are the hot ones; among the rows of one device each hot expert is named exactly 32 times, no row names two hot experts, every other expert is named at most 36 times, and one expert below 8 is named exactly 36 times in the rows of every device.
All inputs are finite; a program needn't handle non-finite values.
Results may differ from a plain program's by a relative error of at most 0.014.
Values may be sent and summed in bfloat16 or wider, within the bound.
A program may use at most 128 MiB of HBM per device.

v0:
```python
import jax
import jax.numpy as jnp
from jax import lax
from jax.sharding import PartitionSpec as P


def forward_rows(rows_x, w_gate, w_up, w_down):
    last_pair = (((1,), (1,)), ((), ()))
    pre_gate = lax.dot_general(rows_x, w_gate, last_pair, preferred_element_type=jnp.float32)
    pre_up = lax.dot_general(rows_x, w_up, last_pair, preferred_element_type=jnp.float32)
    sigma = jax.nn.sigmoid(pre_gate)
    act = (pre_gate * sigma * pre_up).astype(jnp.bfloat16)
    out_part = jnp.dot(act, w_down, preferred_element_type=jnp.float32)
    return (pre_gate, pre_up, act, out_part)


def slopes(rows_d, pre_gate, pre_up, w_down):
    last_pair = (((1,), (1,)), ((), ()))
    d_act = lax.dot_general(rows_d, w_down, last_pair, preferred_element_type=jnp.float32)
    sigma = jax.nn.sigmoid(pre_gate)
    slope = sigma * (1.0 + pre_gate * (1.0 - sigma))
    d_gate = (d_act * pre_up * slope).astype(jnp.bfloat16)
    d_up = (d_act * pre_gate * sigma).astype(jnp.bfloat16)
    return (d_gate, d_up)


def hot_backward(rows_x, rows_d, pre_gate, pre_up, act, w_gate, w_up, w_down):
    first_pair = (((0,), (0,)), ((), ()))
    d_gate, d_up = slopes(rows_d, pre_gate, pre_up, w_down)
    dx_part = jnp.dot(d_gate, w_gate, preferred_element_type=jnp.float32)
    dx_part = dx_part + jnp.dot(d_up, w_up, preferred_element_type=jnp.float32)
    grad_gate = lax.dot_general(d_gate, rows_x, first_pair, preferred_element_type=jnp.float32)
    grad_up = lax.dot_general(d_up, rows_x, first_pair, preferred_element_type=jnp.float32)
    grad_down = lax.dot_general(act, rows_d, first_pair, preferred_element_type=jnp.float32)
    return (dx_part, grad_gate, grad_up, grad_down)


def local(
    tokens,
    cotangent,
    route_ids,
    route_weights,
    cold_gate,
    cold_up,
    cold_down,
    hot_gate,
    hot_up,
    hot_down,
):
    tok_rows, model_width = tokens.shape
    top_count = route_ids.shape[1]
    owners = lax.axis_size("expert")
    replicas = lax.axis_size("dp")
    hot_count = hot_gate.shape[0]
    hot_load = tok_rows // 4
    cold_slots = tok_rows * top_count - hot_count * hot_load
    capacity = max(2, 5 * cold_slots // (4 * owners) + 1)
    pair_count = tok_rows * top_count
    flat_ids = route_ids.reshape(pair_count)
    pair_gain = route_weights.reshape(pair_count)
    onehot = (flat_ids[:, None] == jnp.arange(owners + hot_count, dtype=jnp.int32)[None, :]).astype(
        jnp.int32
    )
    slot_rank = jnp.sum((jnp.cumsum(onehot, axis=0) - onehot) * onehot, axis=1)
    cold_total = owners * capacity
    target = jnp.where(
        flat_ids < owners,
        flat_ids * capacity + slot_rank,
        cold_total + (flat_ids - owners) * hot_load + slot_rank,
    )
    slot_total = cold_total + hot_count * hot_load
    placing = (jnp.arange(slot_total, dtype=jnp.int32)[:, None] == target[None, :]).astype(
        jnp.bfloat16
    )
    x_pairs = jnp.repeat(tokens, top_count, axis=0)
    d_pairs = (
        pair_gain[:, None] * jnp.repeat(cotangent, top_count, axis=0).astype(jnp.float32)
    ).astype(jnp.bfloat16)
    send_x = jnp.dot(placing, x_pairs, preferred_element_type=jnp.float32).astype(jnp.bfloat16)
    send_d = jnp.dot(placing, d_pairs, preferred_element_type=jnp.float32).astype(jnp.bfloat16)
    cold_x = send_x[:cold_total].reshape(owners, capacity, model_width)
    cold_d = send_d[:cold_total].reshape(owners, capacity, model_width)
    hot_x = send_x[cold_total:].reshape(hot_count, hot_load, model_width)
    hot_d = send_d[cold_total:].reshape(hot_count, hot_load, model_width)
    hot_xrows, hot_drows = (
        lax.all_gather(hot_x, "dp", axis=1, tiled=True),
        lax.all_gather(hot_d, "dp", axis=1, tiled=True),
    )
    arrived_x, arrived_d = (
        lax.all_to_all(cold_x, "expert", split_axis=0, concat_axis=0, tiled=True),
        lax.all_to_all(cold_d, "expert", split_axis=0, concat_axis=0, tiled=True),
    )
    hot_fwd = jax.vmap(forward_rows)(hot_xrows, hot_gate, hot_up, hot_down)
    hot_bwd = jax.vmap(hot_backward)(
        hot_xrows, hot_drows, hot_fwd[0], hot_fwd[1], hot_fwd[2], hot_gate, hot_up, hot_down
    )
    hot_gate_grad, hot_up_grad, hot_down_grad = (
        lax.psum_scatter(hot_bwd[1], "expert", scatter_dimension=2, tiled=True),
        lax.psum_scatter(hot_bwd[2], "expert", scatter_dimension=2, tiled=True),
        lax.psum_scatter(hot_bwd[3], "expert", scatter_dimension=2, tiled=True),
    )
    last_pair = (((1,), (1,)), ((), ()))
    first_pair = (((0,), (0,)), ((), ()))
    full_gate, full_up, full_down = (
        lax.all_gather(cold_gate, "dp", axis=1, tiled=True),
        lax.all_gather(cold_up, "dp", axis=1, tiled=True),
        lax.all_gather(cold_down, "dp", axis=1, tiled=True),
    )
    w_gate = full_gate[0]
    w_up = full_up[0]
    w_down = full_down[0]
    rows_x = arrived_x.reshape(-1, model_width)
    rows_d = arrived_d.reshape(-1, model_width)
    hidden_units = w_gate.shape[0]
    quarter = hidden_units // replicas
    pre_gate = lax.dot_general(rows_x, w_gate, last_pair, preferred_element_type=jnp.float32)
    pre_up = lax.dot_general(rows_x, w_up, last_pair, preferred_element_type=jnp.float32)
    sigma = jax.nn.sigmoid(pre_gate)
    act = (pre_gate * sigma * pre_up).astype(jnp.bfloat16)
    out_q = jnp.einsum(
        "rqf,qfd->rqd",
        act.reshape(-1, replicas, quarter),
        w_down.reshape(replicas, quarter, model_width),
        preferred_element_type=jnp.float32,
    ).astype(jnp.bfloat16)
    cold_out = jnp.sum(out_q.astype(jnp.float32), axis=1).astype(jnp.bfloat16)
    d_gate, d_up = slopes(rows_d, pre_gate, pre_up, w_down)
    dx_gate = jnp.einsum(
        "rqf,qfd->rqd",
        d_gate.reshape(-1, replicas, quarter),
        w_gate.reshape(replicas, quarter, model_width),
        preferred_element_type=jnp.float32,
    )
    dx_up = jnp.einsum(
        "rqf,qfd->rqd",
        d_up.reshape(-1, replicas, quarter),
        w_up.reshape(replicas, quarter, model_width),
        preferred_element_type=jnp.float32,
    )
    dx_q = (dx_gate + dx_up).astype(jnp.bfloat16)
    cold_dx = jnp.sum(dx_q.astype(jnp.float32), axis=1).astype(jnp.bfloat16)
    term_gate = lax.dot_general(d_gate, rows_x, first_pair, preferred_element_type=jnp.float32)
    term_up = lax.dot_general(d_up, rows_x, first_pair, preferred_element_type=jnp.float32)
    term_down = lax.dot_general(act, rows_d, first_pair, preferred_element_type=jnp.float32)
    sum_gate, sum_up, sum_down = (
        lax.psum_scatter(
            term_gate.astype(jnp.bfloat16), "dp", scatter_dimension=0, tiled=True
        ).astype(jnp.float32),
        lax.psum_scatter(
            term_up.astype(jnp.bfloat16), "dp", scatter_dimension=0, tiled=True
        ).astype(jnp.float32),
        lax.psum_scatter(
            term_down.astype(jnp.bfloat16), "dp", scatter_dimension=0, tiled=True
        ).astype(jnp.float32),
    )
    grad_gate = sum_gate.astype(jnp.bfloat16)
    grad_up = sum_up.astype(jnp.bfloat16)
    grad_down = sum_down.astype(jnp.bfloat16)
    hot_sum, hot_dsum = (
        lax.psum_scatter(
            hot_fwd[3].astype(jnp.bfloat16), "dp", scatter_dimension=1, tiled=True
        ).astype(jnp.float32),
        lax.psum_scatter(
            hot_bwd[0].astype(jnp.bfloat16), "dp", scatter_dimension=1, tiled=True
        ).astype(jnp.float32),
    )
    cold_back, cold_dback = (
        lax.all_to_all(
            cold_out.reshape(owners, capacity, model_width),
            "expert",
            split_axis=0,
            concat_axis=0,
            tiled=True,
        ),
        lax.all_to_all(
            cold_dx.reshape(owners, capacity, model_width),
            "expert",
            split_axis=0,
            concat_axis=0,
            tiled=True,
        ),
    )
    hot_out = hot_sum.astype(jnp.bfloat16)
    hot_dx = hot_dsum.astype(jnp.bfloat16)
    back_outs = jnp.concatenate(
        [cold_back.reshape(cold_total, model_width), hot_out.reshape(-1, model_width)], axis=0
    )
    back_grads = jnp.concatenate(
        [cold_dback.reshape(cold_total, model_width), hot_dx.reshape(-1, model_width)], axis=0
    )
    expert_out = lax.dot_general(
        placing, back_outs, first_pair, preferred_element_type=jnp.float32
    ).reshape(tok_rows, top_count, model_width)
    dx_pair = lax.dot_general(
        placing, back_grads, first_pair, preferred_element_type=jnp.float32
    ).reshape(tok_rows, top_count, model_width)
    mixed = jnp.sum(route_weights[:, :, None] * expert_out, axis=1).astype(jnp.bfloat16)
    route_grad = jnp.sum(cotangent.astype(jnp.float32)[:, None, :] * expert_out, axis=2)
    token_grad = jnp.sum(dx_pair, axis=1).astype(jnp.bfloat16)
    return (
        mixed,
        token_grad,
        route_grad,
        grad_gate[None],
        grad_up[None],
        grad_down[None],
        hot_gate_grad,
        hot_up_grad,
        hot_down_grad,
    )


def solution(mesh):
    return jax.shard_map(
        local,
        mesh=mesh,
        in_specs=(
            P(("expert", "dp"), None),
            P(("expert", "dp"), None),
            P(("expert", "dp"), None),
            P(("expert", "dp"), None),
            P("expert", "dp", None),
            P("expert", "dp", None),
            P("expert", "dp", None),
            P(None, "dp", None),
            P(None, "dp", None),
            P(None, "dp", None),
        ),
        out_specs=(
            P(("expert", "dp"), None),
            P(("expert", "dp"), None),
            P(("expert", "dp"), None),
            P("expert", "dp", None),
            P("expert", "dp", None),
            P("expert", "dp", None),
            P(None, "dp", "expert"),
            P(None, "dp", "expert"),
            P(None, "dp", "expert"),
        ),
        check_vma=False,
    )
```

profile of v0, /device:TPU:13, one launch (start us, length us, event | category | flops | bytes accessed | tf_op | source)
XLA Modules:
  0.0 514.7 jit_solution(12889565931586894732)
XLA Ops:
  13.0 1.7 convolution_convert_fusion.4
  15.9 2.4 broadcast_in_dim.21
  18.3 2.8 convert_element_type.105
  22.0 11.1 %all-gather = bf16[128,2048]{1,0:T(8,128)(2,1)S(1)} all-gather(bf16[32,2048]{1,0:T(8,128)(2,1)S(1)} %copy-done.12), channel_id=2, replica_groups=mesh['expert'=8,'dp'=4] {'dp'}, dimensions={0}, use_global_device_ids=true | all-gather | bytes 655360 | tf_op jit(solution)/shard_map/all_gather | solution.py:86
  33.1 10.5 %all-gather.1 = bf16[128,2048]{1,0:T(8,128)(2,1)S(1)} all-gather(bf16[32,2048]{1,0:T(8,128)(2,1)S(1)} %slice.28), channel_id=3, replica_groups=mesh['expert'=8,'dp'=4] {'dp'}, dimensions={0}, use_global_device_ids=true | all-gather | bytes 655360 | tf_op jit(solution)/shard_map/all_gather | solution.py:87
  48.8 2.3 fusion.8
  51.2 1.5 convolution_bitcast_fusion
  52.8 1.5 convolution_bitcast_fusion.1
  54.3 2.5 slice.25
  56.8 2.3 reshape.185
  59.1 5.6 %all-to-all-start = ((bf16[8,36,2048]{2,1,0:T(8,128)(2,1)}), bf16[8,36,2048]{2,1,0:T(8,128)(2,1)}, u32[]{:S(2)}, u32[]{:S(2)}) async-start(bf16[8,36,2048]{2,1,0:T(8,128)(2,1)} %reshape.185), calls=%async_computation | async-start | bytes 2621440 | tf_op jit(solution)/shard_map/all_to_all | solution.py:90
  64.8 2.4 slice.27
  67.2 2.3 reshape.197
  69.5 24.1 %all-to-all-done = bf16[8,36,2048]{2,1,0:T(8,128)(2,1)} async-done(((bf16[8,36,2048]{2,1,0:T(8,128)(2,1)}), bf16[8,36,2048]{2,1,0:T(8,128)(2,1)}, u32[]{:S(2)}, u32[]{:S(2)}) %all-to-all-start) | async-done | bytes 1179680 | tf_op jit(solution)/shard_map/all_to_all | solution.py:90
  93.6 6.5 %all-to-all-start.2 = ((bf16[8,36,2048]{2,1,0:T(8,128)(2,1)}), bf16[8,36,2048]{2,1,0:T(8,128)(2,1)}, u32[]{:S(2)}, u32[]{:S(2)}) async-start(bf16[8,36,2048]{2,1,0:T(8,128)(2,1)} %reshape.197), calls=%async_computation.3 | async-start | bytes 2621440 | tf_op jit(solution)/shard_map/all_to_all | solution.py:91
  100.1 1.5 convolution_bitcast_fusion.2
  101.9 2.2 reshape.186
  104.1 24.9 %all-to-all-done.2 = bf16[8,36,2048]{2,1,0:T(8,128)(2,1)} async-done(((bf16[8,36,2048]{2,1,0:T(8,128)(2,1)}), bf16[8,36,2048]{2,1,0:T(8,128)(2,1)}, u32[]{:S(2)}, u32[]{:S(2)}) %all-to-all-start.2) | async-done | bytes 1179680 | tf_op jit(solution)/shard_map/all_to_all | solution.py:91
  128.9 2.3 reshape.198
  131.2 4.3 fusion.3
  135.5 4.3 fusion.5
  139.8 4.3 multiply_convert_fusion.2
  145.0 3.5 convolution_convert_fusion
  148.5 4.8 convolution_convert_fusion.2
  153.4 4.8 convolution_convert_fusion.1
  159.7 4.6 convert_reduce_fusion
  164.2 2.4 reshape.188
  166.6 6.4 %all-to-all-start.1 = ((bf16[8,36,2048]{2,1,0:T(8,128)(2,1)}), bf16[8,36,2048]{2,1,0:T(8,128)(2,1)}, u32[]{:S(2)}, u32[]{:S(2)}) async-start(bf16[8,36,2048]{2,1,0:T(8,128)(2,1)} %reshape.188), calls=%async_computation.1 | async-start | bytes 2621440 | tf_op jit(solution)/shard_map/all_to_all | solution.py:168
  173.6 1.6 reshape.199
  175.2 3.5 fusion.30
  178.7 2.7 fusion
  181.3 2.2 reshape.201
  183.6 25.8 %all-to-all-done.1 = bf16[8,36,2048]{2,1,0:T(8,128)(2,1)} async-done(((bf16[8,36,2048]{2,1,0:T(8,128)(2,1)}), bf16[8,36,2048]{2,1,0:T(8,128)(2,1)}, u32[]{:S(2)}, u32[]{:S(2)}) %all-to-all-start.1) | async-done | bytes 1179680 | tf_op jit(solution)/shard_map/all_to_all | solution.py:168
  209.4 7.0 %all-to-all-start.3 = ((bf16[8,36,2048]{2,1,0:T(8,128)(2,1)}), bf16[8,36,2048]{2,1,0:T(8,128)(2,1)}, u32[]{:S(2)}, u32[]{:S(2)}) async-start(bf16[8,36,2048]{2,1,0:T(8,128)(2,1)} %reshape.201), calls=%async_computation.4 | async-start | bytes 2621440 | tf_op jit(solution)/shard_map/all_to_all | solution.py:175
  216.4 2.3 reshape.189
  218.6 3.4 multiply_reduce_fusion
  222.9 2.5 reshape.196
  225.4 26.2 %all-to-all-done.3 = bf16[8,36,2048]{2,1,0:T(8,128)(2,1)} async-done(((bf16[8,36,2048]{2,1,0:T(8,128)(2,1)}), bf16[8,36,2048]{2,1,0:T(8,128)(2,1)}, u32[]{:S(2)}, u32[]{:S(2)}) %all-to-all-start.3) | async-done | bytes 1179680 | tf_op jit(solution)/shard_map/all_to_all | solution.py:175
  251.6 2.2 reshape.202
  253.8 3.4 fusion.14
  257.2 3.6 reshape.206
  260.8 5.0 reduce_sum.66
  265.8 3.9 multiply_reduce_fusion.1
  269.7 45.4 %reduce-scatter.21.cloned.1.call-done = f32[1,192,256]{2,1,0:T(8,128)} async-done(((f32[1,192,2048]{2,1,0:T(8,128)}), f32[1,192,256]{2,1,0:T(8,128)}) %reduce-scatter.21.cloned.1.call-update) | async-done | bytes 196624 | tf_op jit(solution)/shard_map/reduce_scatter | solution.py:99
  315.1 69.1 %reduce-scatter.19.cloned.1.call-done = f32[1,192,256]{2,1,0:T(8,128)} async-done(((f32[1,192,2048]{2,1,0:T(8,128)}), f32[1,192,256]{2,1,0:T(8,128)}) %reduce-scatter.19.cloned.1.call-update) | async-done | bytes 196624 | tf_op jit(solution)/shard_map/reduce_scatter | solution.py:98
  384.1 42.1 %reduce-scatter.17.cloned.1.call-done = bf16[192,2048]{1,0:T(8,128)(2,1)} async-done(((bf16[768,2048]{1,0:T(8,128)(2,1)}), bf16[192,2048]{1,0:T(8,128)(2,1)}) %reduce-scatter.17.cloned.1.call-update) | async-done | bytes 786448 | tf_op jit(solution)/shard_map/reduce_scatter | solution.py:152
  426.3 40.9 %reduce-scatter.13.cloned.1.call-done = bf16[192,2048]{1,0:T(8,128)(2,1)} async-done(((bf16[768,2048]{1,0:T(8,128)(2,1)}), bf16[192,2048]{1,0:T(8,128)(2,1)}) %reduce-scatter.13.cloned.1.call-update) | async-done | bytes 786448 | tf_op jit(solution)/shard_map/reduce_scatter | solution.py:146
  467.1 41.0 %reduce-scatter.15.cloned.1.call-done = bf16[192,2048]{1,0:T(8,128)(2,1)} async-done(((bf16[768,2048]{1,0:T(8,128)(2,1)}), bf16[192,2048]{1,0:T(8,128)(2,1)}) %reduce-scatter.15.cloned.1.call-update) | async-done | bytes 786448 | tf_op jit(solution)/shard_map/reduce_scatter | solution.py:149
  (104 shorter events, 16.9 us)
Async XLA Ops:
  7.2 37.3 %copy-start = (bf16[1,192,2048]{2,1,0:T(8,128)(2,1)S(1)}, bf16[1,192,2048]{2,1,0:T(8,128)(2,1)}, u32[]{:S(2)}) copy-start(bf16[1,192,2048]{2,1,0:T(8,128)(2,1)} %param.19) | copy-start | bytes 2359300
  7.2 2.3 copy-start.21
  7.2 3.6 copy-start.22
  7.2 3.9 copy-start.10
  7.2 124.0 %all-gather.8.cloned.1.call-start = ((), (), s32[]{:S(2)}) async-start(), calls=%async_computation.13 | async-start | bytes 3932160 | tf_op jit(solution)/shard_map/all_gather | solution.py:106
  8.0 127.6 %all-gather.6.cloned.1.call-start = ((), (), s32[]{:S(2)}) async-start(), calls=%async_computation.12 | async-start | bytes 3932160 | tf_op jit(solution)/shard_map/all_gather | solution.py:105
  8.7 131.1 %all-gather.10.cloned.1.call-start = ((), (), s32[]{:S(2)}) async-start(), calls=%async_computation.14 | async-start | bytes 3932160 | tf_op jit(solution)/shard_map/all_gather | solution.py:107
  9.4 209.2 %reduce-scatter.9.cloned.1.call-start = ((), (), s32[]{:S(2)}) async-start(), calls=%async_computation.15 | async-start | bytes 655360 | tf_op jit(solution)/shard_map/reduce_scatter | solution.py:160
  11.7 4.2 copy-start.11
  14.8 1.2 copy-start.3
  21.1 0.9 copy-start.12
  21.1 22.6 %copy-start.6 = (bf16[1,192,2048]{2,1,0:T(8,128)(2,1)S(1)}, bf16[1,192,2048]{2,1,0:T(8,128)(2,1)}, u32[]{:S(2)}) copy-start(bf16[1,192,2048]{2,1,0:T(8,128)(2,1)} %param.18) | copy-start | bytes 2359300
  21.7 22.8 %copy-start.2 = (bf16[320,2048]{1,0:T(8,128)(2,1)}, bf16[320,2048]{1,0:T(8,128)(2,1)S(1)}, u32[]{:S(2)}) copy-start(bf16[320,2048]{1,0:T(8,128)(2,1)S(1)} %convolution_convert_fusion.3) | copy-start | bytes 3932164
  21.7 22.3 %copy-start.5 = (bf16[1,192,2048]{2,1,0:T(8,128)(2,1)S(1)}, bf16[1,192,2048]{2,1,0:T(8,128)(2,1)}, u32[]{:S(2)}) copy-start(bf16[1,192,2048]{2,1,0:T(8,128)(2,1)} %param.17) | copy-start | bytes 2359300
  43.7 1.8 copy-start.7
  45.5 0.6 copy-start.19
  47.2 1.6 copy-start.18
  47.2 206.5 %reduce-scatter.11.cloned.1.call-start = ((), (), s32[]{:S(2)}) async-start(), calls=%async_computation.16 | async-start | bytes 655360 | tf_op jit(solution)/shard_map/reduce_scatter | solution.py:163
  47.3 3.9 copy-start.8
  47.3 3.9 copy-start.20
  51.1 218.6 %reduce-scatter.23.cloned.1.call-start = ((), (), s32[]{:S(2)}) async-start(), calls=%async_computation.22 | async-start | bytes 1769472 | tf_op jit(solution)/shard_map/reduce_scatter | solution.py:100
  52.7 262.3 %reduce-scatter.21.cloned.1.call-start = ((), (), s32[]{:S(2)}) async-start(), calls=%async_computation.21 | async-start | bytes 1769472 | tf_op jit(solution)/shard_map/reduce_scatter | solution.py:99
  59.1 34.5 %all-to-all-start = ((bf16[8,36,2048]{2,1,0:T(8,128)(2,1)}), bf16[8,36,2048]{2,1,0:T(8,128)(2,1)}, u32[]{:S(2)}, u32[]{:S(2)}) async-start(bf16[8,36,2048]{2,1,0:T(8,128)(2,1)} %reshape.185), calls=%async_computation | async-start | bytes 2621440 | tf_op jit(solution)/shard_map/all_to_all | solution.py:90
  93.6 35.3 %all-to-all-start.2 = ((bf16[8,36,2048]{2,1,0:T(8,128)(2,1)}), bf16[8,36,2048]{2,1,0:T(8,128)(2,1)}, u32[]{:S(2)}, u32[]{:S(2)}) async-start(bf16[8,36,2048]{2,1,0:T(8,128)(2,1)} %reshape.197), calls=%async_computation.3 | async-start | bytes 2621440 | tf_op jit(solution)/shard_map/all_to_all | solution.py:91
  100.1 284.1 %reduce-scatter.19.cloned.1.call-start = ((), (), s32[]{:S(2)}) async-start(), calls=%async_computation.20 | async-start | bytes 1769472 | tf_op jit(solution)/shard_map/reduce_scatter | solution.py:98
  101.6 324.6 %reduce-scatter.17.cloned.1.call-start = ((), (), s32[]{:S(2)}) async-start(), calls=%async_computation.19 | async-start | bytes 3932160 | tf_op jit(solution)/shard_map/reduce_scatter | solution.py:152
  139.8 5.2 %copy-start.9 = (bf16[288,2048]{1,0:T(8,128)(2,1)S(1)}, bf16[288,2048]{1,0:T(8,128)(2,1)}, u32[]{:S(2)}) copy-start(bf16[288,2048]{1,0:T(8,128)(2,1)} %reshape.198) | copy-start | bytes 3538948
  144.2 0.8 copy-start.16
  144.2 4.3 copy-start.13
  144.2 9.2 %copy-start.14 = (bf16[288,768]{1,0:T(8,128)(2,1)}, bf16[288,768]{1,0:T(8,128)(2,1)S(1)}, u32[]{:S(2)}) copy-start(bf16[288,768]{1,0:T(8,128)(2,1)S(1)} %get-tuple-element.18) | copy-start | bytes 1327108
  148.5 318.7 %reduce-scatter.13.cloned.1.call-start = ((), (), s32[]{:S(2)}) async-start(), calls=%async_computation.17 | async-start | bytes 3932160 | tf_op jit(solution)/shard_map/reduce_scatter | solution.py:146
  153.3 354.8 %reduce-scatter.15.cloned.1.call-start = ((), (), s32[]{:S(2)}) async-start(), calls=%async_computation.18 | async-start | bytes 3932160 | tf_op jit(solution)/shard_map/reduce_scatter | solution.py:149
  158.2 1.0 copy-start.17
  164.2 8.8 %copy-start.15 = (bf16[288,768]{1,0:T(8,128)(2,1)S(1)}, bf16[288,768]{1,0:T(8,128)(2,1)}, u32[]{:S(2)}) copy-start(bf16[288,768]{1,0:T(8,128)(2,1)} %copy-done.14) | copy-start | bytes 1327108
  166.6 42.7 %all-to-all-start.1 = ((bf16[8,36,2048]{2,1,0:T(8,128)(2,1)}), bf16[8,36,2048]{2,1,0:T(8,128)(2,1)}, u32[]{:S(2)}, u32[]{:S(2)}) async-start(bf16[8,36,2048]{2,1,0:T(8,128)(2,1)} %reshape.188), calls=%async_computation.1 | async-start | bytes 2621440 | tf_op jit(solution)/shard_map/all_to_all | solution.py:168
  175.2 3.5 copy-start.4
  209.4 42.2 %all-to-all-start.3 = ((bf16[8,36,2048]{2,1,0:T(8,128)(2,1)}), bf16[8,36,2048]{2,1,0:T(8,128)(2,1)}, u32[]{:S(2)}, u32[]{:S(2)}) async-start(bf16[8,36,2048]{2,1,0:T(8,128)(2,1)} %reshape.201), calls=%async_computation.4 | async-start | bytes 2621440 | tf_op jit(solution)/shard_map/all_to_all | solution.py:175
  257.2 251.0 %copy-start.1 = (bf16[1,192,2048]{2,1,0:T(8,128)(2,1)S(1)}, bf16[1,192,2048]{2,1,0:T(8,128)(2,1)}, u32[]{:S(2)}) copy-start(bf16[1,192,2048]{2,1,0:T(8,128)(2,1)} %param.19) | copy-start | bytes 2359300
Sparse Core Ops, SparseCore 0:
  9.6 35.6 all-gather.7
  46.9 28.4 all-gather.5
  76.9 28.4 all-gather.9
  108.4 21.0 reduce-scatter.8
  132.4 21.6 reduce-scatter.10
  158.0 86.5 reduce-scatter.22
  248.6 66.4 reduce-scatter.20
  319.1 65.0 reduce-scatter.18
  387.3 38.9 reduce-scatter.16
  429.2 37.8 reduce-scatter.12
  470.3 37.8 reduce-scatter.14
where the time goes:
time: 518 us; the launch traced here: 515 us
  waiting for transfers between devices  342 us (66%)
  matrix products  57.1 us (11%)
  local copies, waits for them, and re-layouts  44.3 us (9%)
  starting transfers between devices  26.1 us (5%)
  blocking collectives  21.7 us (4%)
  between operations  14.3 us (3%)
  other arithmetic  9.64 us (2%)
    reduce_scatter x1, waiting for transfers between devices, local(): lax.psum_scatter(hot_bwd[1], 'expert', scatter_dimension=2, tiled=True)  69.1 us
    reduce_scatter x1, waiting for transfers between devices, local(): lax.psum_scatter(hot_bwd[2], 'expert', scatter_dimension=2, tiled=True)  45.4 us
    reduce_scatter x1, waiting for transfers between devices, local(): lax.psum_scatter(term_down.astype(jnp.bfloat16), 'dp', scatter_dimension=...  42.1 us
    reduce_scatter x1, waiting for transfers between devices, local(): lax.psum_scatter(term_up.astype(jnp.bfloat16), 'dp', scatter_dimension=0,...  41 us
    reduce_scatter x1, waiting for transfers between devices, local(): lax.psum_scatter(term_gate.astype(jnp.bfloat16), 'dp', scatter_dimension=...  40.9 us
    all_to_all x1, waiting for transfers between devices, local(): lax.all_to_all(cold_dx.reshape(owners, capacity, model_width), 'expert',...  26.2 us
    all_to_all x1, waiting for transfers between devices, local(): lax.all_to_all(cold_out.reshape(owners, capacity, model_width), 'expert',...  25.8 us
    all_to_all x1, waiting for transfers between devices, local(): lax.all_to_all(cold_d, 'expert', split_axis=0, concat_axis=0, tiled=True)  24.9 us
  transfers between devices with their start and end apart: 15, of which 9 were waited for; matrix products, arithmetic and copies ran while one was open for 21% of the time, Pallas kernels for 0%

commit v1 on v0

v1 whole, which is shorter than its diff:
```python
import functools

import jax
import jax.numpy as jnp
from jax import lax
from jax.experimental import pallas as pl
from jax.experimental.pallas import tpu as pltpu
from jax.sharding import PartitionSpec as P

F32 = jnp.float32
BF16 = jnp.bfloat16
MESH = pl.DeviceIdType.MESH
ROWS = (((1,), (1,)), ((), ()))
COLS = (((0,), (0,)), ((), ()))


def place(axis):
    size = lax.axis_size(axis)
    me = lax.axis_index(axis)
    return me, me // 2, lax.rem(me, 2), size // 2


def remote(src, dst, send, recv, axis, index):
    return pltpu.make_async_remote_copy(
        src_ref=src,
        dst_ref=dst,
        send_sem=send,
        recv_sem=recv,
        device_id={axis: index},
        device_id_type=MESH,
    )


def greet(pairs_axes, all_axes):
    barrier = pltpu.get_barrier_semaphore()
    count = 0
    for axis in pairs_axes:
        me, half, side, halves = place(axis)
        targets = [half * 2 + 1 - side]
        targets += [lax.rem(half + j, halves) * 2 + side for j in range(1, halves)]
        for index in targets:
            pl.semaphore_signal(barrier, inc=1, device_id={axis: index}, device_id_type=MESH)
        count += len(targets)
    for axis in all_axes:
        me, size = lax.axis_index(axis), lax.axis_size(axis)
        for j in range(1, size):
            pl.semaphore_signal(
                barrier, inc=1, device_id={axis: lax.rem(me + j, size)}, device_id_type=MESH
            )
        count += size - 1
    pl.semaphore_wait(barrier, count)


def swap_starts(ins, outs, send, recv):
    me, size = lax.axis_index("expert"), lax.axis_size("expert")
    started = []
    for j in range(1, size):
        for i, (src, dst) in enumerate(zip(ins, outs)):
            other = lax.rem(me + j, size)
            copy = remote(
                src.at[other], dst.at[me], send.at[i, j - 1], recv.at[i, j - 1], "expert", other
            )
            copy.start()
            started.append(copy)
    return started


def dispatch_kernel(gathered, swapped, *refs):
    ag_in, refs = refs[:gathered], refs[gathered:]
    sw_in, refs = refs[:swapped], refs[swapped:]
    ag_out, refs = refs[:gathered], refs[gathered:]
    sw_out, refs = refs[:swapped], refs[swapped:]
    ag_own, refs = refs[:gathered], refs[gathered:]
    sw_own, refs = refs[:swapped], refs[swapped:]
    own_sem, side_send, side_recv, far_send, far_recv, fwd_send, fwd_recv, sw_send, sw_recv = refs
    me, half, side, halves = place("dp")
    rank = lax.axis_index("expert")
    partner = half * 2 + 1 - side
    greet(("dp",), ("expert",))
    far = {}
    for i in range(gathered):
        for j in range(1, halves):
            other = lax.rem(half + j, halves) * 2 + side
            far[i, j] = remote(
                ag_in[i], ag_out[i].at[me], far_send.at[i, j - 1], far_recv.at[i, j - 1], "dp", other
            )
            far[i, j].start()
    swaps = swap_starts(sw_in, sw_out, sw_send, sw_recv)
    sides = []
    for i in range(gathered):
        copy = remote(ag_in[i], ag_out[i].at[me], side_send.at[i], side_recv.at[i], "dp", partner)
        copy.start()
        sides.append(copy)
    loads = []
    for i in range(gathered):
        loads.append((ag_in[i], ag_own[i], ag_out[i].at[me]))
    for i in range(swapped):
        loads.append((sw_in[i].at[rank], sw_own[i], sw_out[i].at[rank]))
    for i, (src, mid, _) in enumerate(loads):
        pltpu.make_async_copy(src, mid, own_sem.at[i]).start()
    for i, (src, mid, dst) in enumerate(loads):
        pltpu.make_async_copy(src, mid, own_sem.at[i]).wait()
        pltpu.make_async_copy(mid, dst, own_sem.at[i]).start()
    forwards = []
    for i in range(gathered):
        for j in range(1, halves):
            far[i, j].wait_recv()
            origin = lax.rem(half + halves - j, halves) * 2 + side
            block = ag_out[i].at[origin]
            copy = remote(
                block, block, fwd_send.at[i, j - 1], fwd_recv.at[i, j - 1], "dp", partner
            )
            copy.start()
            forwards.append(copy)
    for i, (src, mid, dst) in enumerate(loads):
        pltpu.make_async_copy(mid, dst, own_sem.at[i]).wait()
    for copy in far.values():
        copy.wait_send()
    for copy in sides + swaps + forwards:
        copy.wait()


def dispatch(gather, swap):
    ways = lax.axis_size("dp")
    size = lax.axis_size("expert")
    halves = ways // 2
    ng, ns = len(gather), len(swap)
    dma = pltpu.SemaphoreType.DMA
    anywhere = pl.BlockSpec(memory_space=pl.ANY)
    shapes = [jax.ShapeDtypeStruct((ways,) + a.shape, a.dtype) for a in gather]
    shapes += [jax.ShapeDtypeStruct(a.shape, a.dtype) for a in swap]
    outs = pl.pallas_call(
        functools.partial(dispatch_kernel, ng, ns),
        out_shape=shapes,
        in_specs=[anywhere] * (ng + ns),
        out_specs=[anywhere] * (ng + ns),
        scratch_shapes=[pltpu.VMEM(a.shape, a.dtype) for a in gather]
        + [pltpu.VMEM(a.shape[1:], a.dtype) for a in swap]
        + [
            dma((ng + ns,)),
            dma((ng,)),
            dma((ng,)),
            dma((ng, halves - 1)),
            dma((ng, halves - 1)),
            dma((ng, halves - 1)),
            dma((ng, halves - 1)),
            dma((ns, size - 1)),
            dma((ns, size - 1)),
        ],
        compiler_params=pltpu.CompilerParams(
            collective_id=0, has_side_effects=True, vmem_limit_bytes=20 << 20
        ),
        name="dispatch",
    )(*gather, *swap)
    return outs[:ng], outs[ng:]


def add_rows(dst, srcs):
    rows = dst.shape[0]
    step = 16 if rows % 16 == 0 else rows

    def body(i, carry):
        at = pl.ds(pl.multiple_of(i * step, step), step)
        total = srcs[0][at, :].astype(F32)
        for src in srcs[1:]:
            total = total + src[at, :].astype(F32)
        dst[at, :] = total.astype(dst.dtype)
        return carry

    lax.fori_loop(0, rows // step, body, 0)


def combine_kernel(axes, swapped, *refs):
    count = len(axes)
    rs_in, refs = refs[:count], refs[count:]
    sw_in, refs = refs[:swapped], refs[swapped:]
    rs_out, refs = refs[:count], refs[count:]
    sw_out, refs = refs[:swapped], refs[swapped:]
    sw_own, refs = refs[:swapped], refs[swapped:]
    own_sem, sw_send, sw_recv = refs[:3]
    bufs = [refs[3 + 11 * i : 14 + 11 * i] for i in range(count)]
    rank = lax.axis_index("expert")
    greet(("dp",), ("expert",))
    sides, mines = {}, {}
    deepest = max(lax.axis_size(axis) // 2 for axis in axes)
    for turn in range(1, deepest + 1):
        for i, axis in enumerate(axes):
            _, half, side, halves = place(axis)
            if turn > halves:
                continue
            j = turn % halves
            arrived, held, _, _, _, load_sem, s_send, s_recv = bufs[i][:8]
            to = lax.rem(half + j, halves) * 2
            partner = half * 2 + 1 - side
            sides[i, j] = remote(
                rs_in[i].at[to + 1 - side], arrived.at[j], s_send.at[j], s_recv.at[j], axis, partner
            )
            sides[i, j].start()
            mines[i, j] = pltpu.make_async_copy(
                rs_in[i].at[to + side], held.at[j], load_sem.at[j]
            )
            mines[i, j].start()
    swaps = swap_starts(sw_in, sw_out, sw_send, sw_recv)
    for i in range(swapped):
        pltpu.make_async_copy(sw_in[i].at[rank], sw_own[i], own_sem.at[i]).start()
    for i in range(swapped):
        pltpu.make_async_copy(sw_in[i].at[rank], sw_own[i], own_sem.at[i]).wait()
        pltpu.make_async_copy(sw_own[i], sw_out[i].at[rank], own_sem.at[i]).start()
    fars = {}
    for i, axis in enumerate(axes):
        _, half, side, halves = place(axis)
        arrived, held, summed, landed, _, _, _, _, f_send, f_recv, _ = bufs[i]
        for j in range(1, halves):
            sides[i, j].wait_recv()
            mines[i, j].wait()
            add_rows(summed.at[j - 1], [arrived.at[j], held.at[j]])
            other = lax.rem(half + j, halves) * 2 + side
            fars[i, j] = remote(
                summed.at[j - 1], landed.at[j - 1], f_send.at[j - 1], f_recv.at[j - 1], axis, other
            )
            fars[i, j].start()
    puts = []
    for i, axis in enumerate(axes):
        halves = lax.axis_size(axis) // 2
        arrived, held, summed, landed, result, _, _, _, _, _, out_sem = bufs[i]
        sides[i, 0].wait_recv()
        mines[i, 0].wait()
        for j in range(1, halves):
            fars[i, j].wait_recv()
        add_rows(
            result, [arrived.at[0], held.at[0]] + [landed.at[j - 1] for j in range(1, halves)]
        )
        put = pltpu.make_async_copy(result, rs_out[i], out_sem.at[0])
        put.start()
        puts.append(put)
    for i in range(swapped):
        pltpu.make_async_copy(sw_own[i], sw_out[i].at[rank], own_sem.at[i]).wait()
    for copy in list(sides.values()) + list(fars.values()):
        copy.wait_send()
    for copy in swaps + puts:
        copy.wait()


def combine(reduce, swap):
    size = lax.axis_size("expert")
    nr, ns = len(reduce), len(swap)
    dma = pltpu.SemaphoreType.DMA
    anywhere = pl.BlockSpec(memory_space=pl.ANY)
    shapes = [jax.ShapeDtypeStruct(a.shape[1:], kind) for _, a, kind in reduce]
    shapes += [jax.ShapeDtypeStruct(a.shape, a.dtype) for a in swap]
    scratch = [pltpu.VMEM(a.shape[1:], a.dtype) for a in swap]
    scratch += [dma((ns,)), dma((ns, size - 1)), dma((ns, size - 1))]
    for axis, a, kind in reduce:
        halves = lax.axis_size(axis) // 2
        block = a.shape[1:]
        scratch += [
            pltpu.VMEM((halves,) + block, a.dtype),
            pltpu.VMEM((halves,) + block, a.dtype),
            pltpu.VMEM((halves - 1,) + block, a.dtype),
            pltpu.VMEM((halves - 1,) + block, a.dtype),
            pltpu.VMEM(block, kind),
            dma((halves,)),
            dma((halves,)),
            dma((halves,)),
            dma((halves - 1,)),
            dma((halves - 1,)),
            dma((1,)),
        ]
    outs = pl.pallas_call(
        functools.partial(combine_kernel, tuple(axis for axis, _, _ in reduce), ns),
        out_shape=shapes,
        in_specs=[anywhere] * (nr + ns),
        out_specs=[anywhere] * (nr + ns),
        scratch_shapes=scratch,
        compiler_params=pltpu.CompilerParams(
            collective_id=1, has_side_effects=True, vmem_limit_bytes=56 << 20
        ),
        name="combine",
    )(*[a for _, a, _ in reduce], *swap)
    return outs[:nr], outs[nr:]


def dot(a, b, dims=None):
    if dims is None:
        return jnp.dot(a, b, preferred_element_type=F32)
    return lax.dot_general(a, b, dims, preferred_element_type=F32)


def expert_block(rows_x, rows_d, w_gate, w_up, w_down):
    pre_gate = dot(rows_x, w_gate, ROWS)
    pre_up = dot(rows_x, w_up, ROWS)
    sigma = jax.nn.sigmoid(pre_gate)
    act = (pre_gate * sigma * pre_up).astype(BF16)
    out = dot(act, w_down).astype(BF16)
    d_act = dot(rows_d, w_down, ROWS)
    slope = sigma * (1.0 + pre_gate * (1.0 - sigma))
    d_gate = (d_act * pre_up * slope).astype(BF16)
    d_up = (d_act * pre_gate * sigma).astype(BF16)
    dx = (dot(d_gate, w_gate) + dot(d_up, w_up)).astype(BF16)
    return (
        out,
        dx,
        dot(d_gate, rows_x, COLS).astype(BF16),
        dot(d_up, rows_x, COLS).astype(BF16),
        dot(act, rows_d, COLS).astype(BF16),
    )


def local(
    tokens,
    cotangent,
    route_ids,
    route_weights,
    cold_gate,
    cold_up,
    cold_down,
    hot_gate,
    hot_up,
    hot_down,
):
    tok_rows, width = tokens.shape
    top_count = route_ids.shape[1]
    owners = lax.axis_size("expert")
    replicas = lax.axis_size("dp")
    hot_count, hot_units = hot_gate.shape[:2]
    hot_load = tok_rows // 4
    cold_slots = tok_rows * top_count - hot_count * hot_load
    capacity = max(2, 5 * cold_slots // (4 * owners) + 1)
    capacity = (capacity + 7) // 8 * 8
    cold_total = owners * capacity
    hot_rows = hot_count * hot_load
    slot_total = cold_total + hot_rows

    ids_row = route_ids.T
    earlier = lax.broadcasted_iota(jnp.int32, (tok_rows, tok_rows), 0) < lax.broadcasted_iota(
        jnp.int32, (tok_rows, tok_rows), 1
    )
    slots = lax.broadcasted_iota(jnp.int32, (slot_total, tok_rows), 0)
    placing, pieces = [], []
    for k in range(top_count):
        mine = ids_row[k][None, :]
        same = sum((route_ids[:, o][:, None] == mine).astype(jnp.int32) for o in range(top_count))
        rank = jnp.sum(jnp.where(earlier, same, 0), axis=0)[None, :]
        target = jnp.where(
            mine < owners,
            mine * capacity + rank,
            cold_total + (mine - owners) * hot_load + rank,
        )
        hit = slots == target
        placing.append(hit.astype(BF16))
        pieces.append(jnp.where(hit, route_weights[:, k][None, :], 0.0))
    either = sum(placing[1:], placing[0])
    gain = jnp.sum(sum(pieces[1:], pieces[0]), axis=1, keepdims=True)
    send_x = dot(either, tokens).astype(BF16)
    send_d = (gain * dot(either, cotangent)).astype(BF16)

    (g_gate, g_up, g_down, hot_x, hot_d), (cold_x, cold_d) = dispatch(
        (cold_gate[0], cold_up[0], cold_down[0], send_x[cold_total:], send_d[cold_total:]),
        (
            send_x[:cold_total].reshape(owners, capacity, width),
            send_d[:cold_total].reshape(owners, capacity, width),
        ),
    )

    hot_outs, hot_dxs, hot_grads = [], [], []
    for h in range(hot_count):
        rows_x = hot_x[:, h * hot_load : (h + 1) * hot_load].reshape(-1, width)
        rows_d = hot_d[:, h * hot_load : (h + 1) * hot_load].reshape(-1, width)
        out, dx, *grads = expert_block(rows_x, rows_d, hot_gate[h], hot_up[h], hot_down[h])
        hot_outs.append(out.reshape(replicas, hot_load, width))
        hot_dxs.append(dx.reshape(replicas, hot_load, width))
        hot_grads.append(grads)
    hot_out = jnp.concatenate(hot_outs, axis=1)
    hot_dx = jnp.concatenate(hot_dxs, axis=1)
    blocks = [
        jnp.concatenate([grads[m] for grads in hot_grads], axis=0)
        .reshape(hot_count * hot_units, owners, width // owners)
        .transpose(1, 0, 2)
        for m in range(3)
    ]

    out, dx, *terms = expert_block(
        cold_x.reshape(cold_total, width),
        cold_d.reshape(cold_total, width),
        g_gate.reshape(-1, width),
        g_up.reshape(-1, width),
        g_down.reshape(-1, width),
    )
    units = cold_gate.shape[1]
    terms = [term.reshape(replicas, units, width) for term in terms]
    sums, (back_out, back_dx) = combine(
        [("dp", term, BF16) for term in terms]
        + [("dp", hot_out, BF16), ("dp", hot_dx, BF16)]
        + [("expert", block, F32) for block in blocks],
        (out.reshape(owners, capacity, width), dx.reshape(owners, capacity, width)),
    )
    back_outs = jnp.concatenate([back_out.reshape(cold_total, width), sums[3]], axis=0)
    back_grads = jnp.concatenate([back_dx.reshape(cold_total, width), sums[4]], axis=0)
    outs = [dot(p, back_outs, COLS) for p in placing]
    mixed = sum(route_weights[:, k][:, None] * outs[k] for k in range(top_count)).astype(BF16)
    cot = cotangent.astype(F32)
    route_grad = jnp.stack([jnp.sum(cot * o, axis=1) for o in outs], axis=1)
    token_grad = dot(either, back_grads, COLS).astype(BF16)
    hot_sums = [s.reshape(hot_count, hot_units, width // owners) for s in sums[5:]]
    return (mixed, token_grad, route_grad, sums[0][None], sums[1][None], sums[2][None], *hot_sums)


def solution(mesh):
    rows = P(("expert", "dp"), None)
    owned = P("expert", "dp", None)
    hot = P(None, "dp", None)
    hot_out = P(None, "dp", "expert")
    return jax.shard_map(
        local,
        mesh=mesh,
        in_specs=(rows,) * 4 + (owned,) * 3 + (hot,) * 3,
        out_specs=(rows,) * 3 + (owned,) * 3 + (hot_out,) * 3,
        check_vma=False,
    )
```

time: 518 us -> 200 us (0.39)
  waiting for transfers between devices: 342 us -> 0 us
  Pallas kernels: 0 us -> 150 us
  local copies, waits for them, and re-layouts: 44.3 us -> 13.1 us
  starting transfers between devices: 26.1 us -> 0 us
  matrix products: 57.1 us -> 32 us
  blocking collectives: 21.7 us -> 0 us
  between operations: 14.3 us -> 0.9 us
  other arithmetic: 9.64 us -> 1.6 us
    reduce_scatter x8 -> x0, waiting for transfers between devices: 238 us -> none  [the longest x1 69.1 us: local(): lax.psum_scatter(hot_bwd[1], 'expert', scatter_dimension=2, tiled=True)]
    pallas_call x0 -> x2, Pallas kernels: none -> 150 us  [the longest x1 87.7 us: combine(): pl.pallas_call(functools.partial(combine_kernel, tuple((axis for axis, _,...]
    all_to_all x4 -> x0, waiting for transfers between devices: 101 us -> none  [the longest x1 26.2 us: local(): lax.all_to_all(cold_dx.reshape(owners, capacity, model_width), 'expert',...]
    reshape x15 -> x1, local copies, waits for them, and re-layouts: 28.3 us -> 0.93 us  [local(): blocks = [jnp.concatenate([grads[m] for grads in hot_grads], axis=0).resh...]
    all_to_all x4 -> x0, starting transfers between devices: 25.5 us -> none  [the longest x1 7.01 us: local(): lax.all_to_all(cold_dx.reshape(owners, capacity, model_width), 'expert',...]
    dot_general x22 -> x23, matrix products: 57.1 us -> 32 us  [the longest x15 21.5 us: dot(): return lax.dot_general(a, b, dims, preferred_element_type=F32)]
    all_gather x2 -> x0, blocking collectives: 21.7 us -> none  [the longest x1 11.1 us: local(): lax.all_gather(hot_x, 'dp', axis=1, tiled=True)]
    reduce_sum x3 -> x2, other arithmetic: 8.93 us -> 0.26 us  [the longest x1 0.15 us: local(): gain = jnp.sum(sum(pieces[1:], pieces[0]), axis=1, keepdims=True)]
  transfers between devices with their start and end apart: 15 -> 0, of which waited for: 9 -> 0; matrix products, arithmetic and copies ran while one was open for 21% -> 0% of each run, Pallas kernels for 0% -> 0%
where the time goes in v1:
time: 200 us; the launch traced here: 198 us
  Pallas kernels  150 us (75%)
  matrix products  32 us (16%)
  local copies, waits for them, and re-layouts  13.1 us (7%)
    pallas_call x1, Pallas kernels, combine(): pl.pallas_call(functools.partial(combine_kernel, tuple((axis for axis, _,...  87.7 us
    pallas_call x1, Pallas kernels, dispatch(): pl.pallas_call(functools.partial(dispatch_kernel, ng, ns), out_shape=shap...  62.8 us
    dot_general x15, matrix products, dot(): return lax.dot_general(a, b, dims, preferred_element_type=F32)  21.5 us
    dot_general x8, matrix products, dot(): return jnp.dot(a, b, preferred_element_type=F32)  10.4 us
    unnamed x38, local copies, waits for them, and re-layouts  8.31 us

profile of v1, /device:TPU:13, one launch (start us, length us, event | category | flops | bytes accessed | tf_op | source)
XLA Modules:
  0.0 198.1 jit_solution(15191021697146516236)
XLA Ops:
  0.7 0.8 slice_bitcast_fusion.3
  1.4 0.8 slice_bitcast_fusion.4
  2.2 0.8 slice_bitcast_fusion.2
  2.9 0.1 select_reduce_fusion.1
  3.1 0.8 fusion.34
  3.8 0.1 add_reduce_fusion
  4.0 1.6 fusion
  5.6 0.1 slice.47
  5.7 0.9 copy-done.9
  6.6 0.5 convolution_convert_fusion.3
  7.2 0.1 slice.46
  7.3 0.9 copy-done.1
  8.3 0.2 copy-done.2
  8.5 0.2 copy-done.3
  8.7 62.8 %dispatch.1 = (bf16[4,192,2048]{2,1,0:T(8,128)(2,1)S(1)}, bf16[4,192,2048]{2,1,0:T(8,128)(2,1)S(1)}, bf16[4,192,2048]{2,1,0:T(8,128)(2,1)S(1)}, bf16[4,32,2048]{...) custom-call(bf16[192,2048]{1,0:T(8,128)(2,1)S(1)} %bitcast.134, ...), custom_call_target="tpu_custom_call" | custom-call | tf_op jit(solution)/shard_map/dispatch/pallas_call | solution.py:132
  71.5 0.4 fusion.14
  71.9 0.7 copy-done.4
  72.6 0.4 fusion.18
  73.1 0.4 multiply_convert_fusion.3
  73.4 0.4 convolution_convert_fusion.5
  73.8 1.1 convolution_convert_fusion.9
  74.9 0.3 convolution_convert_fusion.6
  75.3 1.3 bitcast_bitcast_fusion
  76.6 0.4 convolution_convert_fusion.7
  76.9 0.9 copy.31
  77.9 1.2 fusion.39
  79.1 1.2 fusion.40
  80.3 1.5 multiply_convert_fusion
  81.8 1.2 fusion.41
  83.0 2.3 %fusion.1 = bf16[320,2048]{1,0:T(8,128)(2,1)} fusion(f32[320,2048]{1,0:T(8,128)S(1)} %fusion.41, bf16[320,768]{1,0:T(8,128)(2,1)S(1)} %get-tuple-element.50, bf16[768,2048]{1,0:T(8,128)(2,1)S(1)} %bitcast.142), kind=kOutput, calls=%fused_computation.7 | convolution fusion | flops 1007943680 | bytes 7569408 | tf_op jit(solution)/shard_map/dot_general | solution.py:285
  85.3 2.3 %convolution_convert_fusion.4 = bf16[320,2048]{1,0:T(8,128)(2,1)} fusion(bf16[320,768]{1,0:T(8,128)(2,1)S(1)} %get-tuple-element.48, bf16[768,2048]{1,0:T(8,128)(2,1)S(1)} %bitcast.140), kind=kOutput, calls=%fused_computation.8 | convolution fusion | flops 1007288320 | bytes 4947968 | tf_op jit(solution)/shard_map/dot_general | solution.py:285
  87.6 0.3 fusion.16
  87.9 1.1 fusion.2
  89.0 3.5 %convolution_convert_fusion = bf16[768,2048]{1,0:T(8,128)(2,1)} fusion(bf16[320,768]{1,0:T(8,128)(2,1)S(1)} %get-tuple-element.48, bf16[320,2048]{1,0:T(8,128)(2,1)S(1)} %bitcast.148), kind=kOutput, calls=%fused_computation | convolution fusion | flops 1008205824 | bytes 4947968 | tf_op jit(solution)/shard_map/dot_general | solution.py:286
  92.6 3.6 %convolution_convert_fusion.2 = bf16[768,2048]{1,0:T(8,128)(2,1)} fusion(bf16[320,768]{1,0:T(8,128)(2,1)S(1)} %get-tuple-element.49, bf16[320,2048]{1,0:T(8,128)(2,1)S(1)} %bitcast.145), kind=kOutput, calls=%fused_computation.2 | convolution fusion | flops 1008205824 | bytes 4947968 | tf_op jit(solution)/shard_map/dot_general | solution.py:286
  96.2 3.5 %convolution_convert_fusion.1 = bf16[768,2048]{1,0:T(8,128)(2,1)} fusion(bf16[320,768]{1,0:T(8,128)(2,1)S(1)} %get-tuple-element.50, bf16[320,2048]{1,0:T(8,128)(2,1)S(1)} %bitcast.146), kind=kOutput, calls=%fused_computation.1 | convolution fusion | flops 1008205824 | bytes 4947968 | tf_op jit(solution)/shard_map/dot_general | solution.py:286
  99.7 87.7 %combine.1 = (bf16[192,2048]{1,0:T(8,128)(2,1)}, bf16[192,2048]{1,0:T(8,128)(2,1)}, bf16[192,2048]{1,0:T(8,128)(2,1)}, bf16[32,2048]{1,0:T(8,128)(2,1)}, bf16[32...) custom-call(bf16[4,192,2048]{2,1,0:T(8,128)(2,1)} %bitcast.153, ...), custom_call_target="tpu_custom_call" | custom-call | tf_op jit(solution)/shard_map/combine/pallas_call | solution.py:269
  187.5 2.8 %convolution_convert_fusion.8 = bf16[128,2048]{1,0:T(8,128)(2,1)} fusion(bf16[32,2048]{1,0:T(8,128)(2,1)} %get-tuple-element.36, bf16[320,2048]{1,0:T(8,128)(2,1)} %bitcast.172, s32[128]{0:T(128)S(1)} %get-tuple-element.57, s32[128]{0:T(128)S(1)} %get-tuple-element.56), kind=kOutput, calls=%fused_computation.14 | convolution fusion | flops 188055552 | bytes 1967104 | tf_op jit(solution)/shard_map/dot_general | solution.py:286
  190.2 0.5 fusion.8
  190.7 0.5 copy-done.10
  191.3 1.5 fusion.6
  192.8 0.6 pad_maximum_fusion.3
  193.4 0.9 copy.38
  194.3 0.9 copy.39
  195.2 0.9 copy.40
  196.0 0.7 copy.41
  196.7 0.7 copy.42
  197.4 0.7 copy.43
  (28 shorter events, 0.1 us)
Async XLA Ops:
  0.6 72.4 %copy-start = (bf16[1,192,2048]{2,1,0:T(8,128)(2,1)S(1)}, bf16[1,192,2048]{2,1,0:T(8,128)(2,1)}, u32[]{:S(2)}) copy-start(bf16[1,192,2048]{2,1,0:T(8,128)(2,1)} %param.19) | copy-start | bytes 2359300
  5.6 1.0 copy-start.9
  7.1 1.1 copy-start.1
  7.1 1.4 copy-start.2
  7.2 1.6 copy-start.3
  8.7 62.8 %copy-start.5 = (bf16[1,192,2048]{2,1,0:T(8,128)(2,1)S(1)}, bf16[1,192,2048]{2,1,0:T(8,128)(2,1)}, u32[]{:S(2)}) copy-start(bf16[1,192,2048]{2,1,0:T(8,128)(2,1)} %param.18) | copy-start | bytes 2359300
  71.5 1.1 copy-start.4
  187.4 2.8 %copy-start.14 = (bf16[8,40,2048]{2,1,0:T(8,128)(2,1)S(1)}, bf16[8,40,2048]{2,1,0:T(8,128)(2,1)}, u32[]{:S(2)}) copy-start(bf16[8,40,2048]{2,1,0:T(8,128)(2,1)} %get-tuple-element.33) | copy-start | bytes 3932164
  187.5 2.8 %copy-start.15 = (bf16[32,2048]{1,0:T(8,128)(2,1)S(1)}, bf16[32,2048]{1,0:T(8,128)(2,1)}, u32[]{:S(2)}) copy-start(bf16[32,2048]{1,0:T(8,128)(2,1)} %get-tuple-element.34) | copy-start | bytes 393220
  190.2 1.0 copy-start.10
  191.3 2.1 %copy-start.8 = (bf16[192,2048]{1,0:T(8,128)(2,1)S(1)}, bf16[192,2048]{1,0:T(8,128)(2,1)}, u32[]{:S(2)}) copy-start(bf16[192,2048]{1,0:T(8,128)(2,1)} %get-tuple-element.37) | copy-start | bytes 2359300
  192.8 1.5 copy-start.7
  193.4 1.8 copy-start.6
  194.3 1.8 copy-start.13
  194.3 2.5 %copy-start.12 = (f32[192,256]{1,0:T(8,128)S(1)}, f32[192,256]{1,0:T(8,128)}, u32[]{:S(2)}) copy-start(f32[192,256]{1,0:T(8,128)} %get-tuple-element.41) | copy-start | bytes 589828
  194.3 3.1 %copy-start.11 = (f32[192,256]{1,0:T(8,128)S(1)}, f32[192,256]{1,0:T(8,128)}, u32[]{:S(2)}) copy-start(f32[192,256]{1,0:T(8,128)} %get-tuple-element.42) | copy-start | bytes 589828

commit v2 on v1

--- a/solution.py
+++ b/solution.py
@@ -306,6 +306,399 @@
     )
 
 
+def mix(pre_gate, pre_up):
+    sigma = 1.0 / (1.0 + jnp.exp(-pre_gate))
+    return sigma, pre_gate * sigma
+
+
+def layer_kernel(*refs):
+    hot_in, cold_in, own_w, hot_w = refs[:2], refs[2:4], refs[4:7], refs[7:10]
+    back, sums, hot_sums, hot_grads = refs[10:12], refs[12:15], refs[15:17], refs[17:20]
+    hot_rows, weights, landing, packed = refs[20:22], refs[22:25], refs[25:27], refs[27:29]
+    pre_g, pre_u, act, d_gate, d_up = refs[29:34]
+    results, terms, hot_parts, hot_terms = refs[34:36], refs[36:39], refs[39:41], refs[41:44]
+    arrived, summed, landed = refs[44:49], refs[49:54], refs[54:59]
+    e_arrived, e_held, e_summed, e_landed = refs[59:62], refs[62:65], refs[65:68], refs[68:71]
+    (own_sem, ag_fs, ag_fr, ag_ss, ag_sr, ag_ws, ag_wr, sw_s, sw_r, bk_s, bk_r) = refs[71:82]
+    (rs_ss, rs_sr, rs_fs, rs_fr, ex_ss, ex_sr, ex_fs, ex_fr, ex_l) = refs[82:91]
+    me, half, side, halves = place("dp")
+    rank, e_half, e_side, e_halves = place("expert")
+    owners = 2 * e_halves
+    partner, e_partner = half * 2 + 1 - side, e_half * 2 + 1 - e_side
+    slots = 2 * halves
+    load, width = hot_in[0].shape
+    cap = cold_in[0].shape[1]
+    part = width // owners
+    tile = 512 if width % 512 == 0 else width
+    pending = []
+
+    def go(copy):
+        copy.start()
+        return copy
+
+    def slot_of(buffer, s):
+        if len(buffer.shape) == 2:
+            return buffer.at[pl.ds(s * load, load)]
+        return buffer.at[s]
+
+    def tiles(body):
+        def step(i, carry):
+            body(pl.ds(pl.multiple_of(i * tile, tile), tile))
+            return carry
+
+        lax.fori_loop(0, width // tile, step, 0)
+
+    greet(("dp",), ("expert",))
+    sources = list(hot_in) + list(own_w)
+    targets = list(hot_rows) + list(weights)
+    far, near, forwarded, own = {}, {}, {}, {}
+
+    def send_near(i):
+        near[i] = go(
+            remote(sources[i], slot_of(targets[i], 1), ag_ss.at[i], ag_sr.at[i], "dp", partner)
+        )
+        own[i] = go(pltpu.make_async_copy(sources[i], slot_of(targets[i], 0), own_sem.at[i]))
+
+    def forward(i):
+        for j in range(1, halves):
+            far[i, j].wait_recv()
+            forwarded[i, j] = go(
+                remote(
+                    slot_of(targets[i], 2 * j),
+                    slot_of(targets[i], 2 * j + 1),
+                    ag_ws.at[i, j - 1],
+                    ag_wr.at[i, j - 1],
+                    "dp",
+                    partner,
+                )
+            )
+
+    for i in range(5):
+        for j in range(1, halves):
+            other = lax.rem(half + j, halves) * 2 + side
+            far[i, j] = go(
+                remote(
+                    sources[i],
+                    slot_of(targets[i], 2 * j),
+                    ag_fs.at[i, j - 1],
+                    ag_fr.at[i, j - 1],
+                    "dp",
+                    other,
+                )
+            )
+    swaps, mine = [], []
+    for i in range(2):
+        for j in range(1, owners):
+            other = lax.rem(rank + j, owners)
+            swaps.append(
+                go(
+                    remote(
+                        cold_in[i].at[other],
+                        landing[i].at[rank],
+                        sw_s.at[i, j - 1],
+                        sw_r.at[i, j - 1],
+                        "expert",
+                        other,
+                    )
+                )
+            )
+        mine.append(
+            go(
+                pltpu.make_async_copy(
+                    cold_in[i].at[rank], landing[i].at[rank], own_sem.at[5 + i]
+                )
+            )
+        )
+    for i in range(5):
+        send_near(i)
+
+    for i in (0, 1):
+        forward(i)
+    for i in (0, 1):
+        near[i].wait_recv()
+        own[i].wait()
+        for j in range(1, halves):
+            forwarded[i, j].wait_recv()
+    w_gate, w_up, w_down = hot_w
+    gate = dot(hot_rows[0][...], w_gate[...], ROWS)
+    up = dot(hot_rows[0][...], w_up[...], ROWS)
+    sigma, silu = mix(gate, up)
+    d_act = dot(hot_rows[1][...], w_down[...], ROWS)
+    h_act = (silu * up).astype(BF16)
+    h_dg = (d_act * up * (sigma * (1.0 + gate * (1.0 - sigma)))).astype(BF16)
+    h_du = (d_act * silu).astype(BF16)
+
+    def hot_tile(at):
+        hot_parts[0][:, at] = dot(h_act, w_down[:, at]).astype(BF16)
+        hot_parts[1][:, at] = (dot(h_dg, w_gate[:, at]) + dot(h_du, w_up[:, at])).astype(BF16)
+        hot_terms[0][:, at] = dot(h_dg, hot_rows[0][:, at], COLS).astype(BF16)
+        hot_terms[1][:, at] = dot(h_du, hot_rows[0][:, at], COLS).astype(BF16)
+        hot_terms[2][:, at] = dot(h_act, hot_rows[1][:, at], COLS).astype(BF16)
+
+    tiles(hot_tile)
+
+    locals_ = list(terms) + list(hot_parts)
+    rs_near, rs_far, ex_near, ex_far, ex_held = {}, {}, {}, {}, {}
+
+    def reduce_near(i, j):
+        rs_near[i, j] = go(
+            remote(
+                slot_of(locals_[i], 2 * j + 1),
+                arrived[i].at[j],
+                rs_ss.at[i, j],
+                rs_sr.at[i, j],
+                "dp",
+                partner,
+            )
+        )
+
+    def reduce_far(i, j):
+        rs_near[i, j].wait_recv()
+        add_rows(summed[i].at[j - 1], [arrived[i].at[j], slot_of(locals_[i], 2 * j)])
+        other = lax.rem(half + halves - j, halves) * 2 + side
+        rs_far[i, j] = go(
+            remote(
+                summed[i].at[j - 1],
+                landed[i].at[j - 1],
+                rs_fs.at[i, j - 1],
+                rs_fr.at[i, j - 1],
+                "dp",
+                other,
+            )
+        )
+
+    def columns(index):
+        return pl.ds(pl.multiple_of(index * part, 128), part)
+
+    for i in range(3):
+        for j in list(range(1, e_halves)) + [0]:
+            to = lax.rem(e_half + j, e_halves) * 2
+            ex_near[i, j] = go(
+                remote(
+                    hot_terms[i].at[:, columns(to + 1 - e_side)],
+                    e_arrived[i].at[j],
+                    ex_ss.at[i, j],
+                    ex_sr.at[i, j],
+                    "expert",
+                    e_partner,
+                )
+            )
+            ex_held[i, j] = go(
+                pltpu.make_async_copy(
+                    hot_terms[i].at[:, columns(to + e_side)], e_held[i].at[j], ex_l.at[i, j]
+                )
+            )
+    for i in (3, 4):
+        for j in range(halves - 1, -1, -1):
+            reduce_near(i, j)
+
+    def repack(i):
+        def step(k, carry):
+            a, b = landing[i][2 * k].astype(F32), landing[i][2 * k + 1].astype(F32)
+            at = pl.ds(pl.multiple_of(k * 2 * cap, 16), 2 * cap)
+            packed[i][at, :] = jnp.concatenate([a, b], axis=0).astype(BF16)
+            return carry
+
+        lax.fori_loop(0, owners // 2, step, 0)
+
+    def give_back(i):
+        for j in range(1, owners):
+            other = lax.rem(rank + j, owners)
+            pending.append(
+                go(
+                    remote(
+                        results[i].at[other],
+                        back[i].at[rank],
+                        bk_s.at[i, j - 1],
+                        bk_r.at[i, j - 1],
+                        "expert",
+                        other,
+                    )
+                )
+            )
+        pending.append(
+            go(pltpu.make_async_copy(results[i].at[rank], back[i].at[rank], own_sem.at[7 + i]))
+        )
+
+    def put_rows(i, at, value):
+        for e in range(owners):
+            results[i][e, :, at] = value[e * cap : (e + 1) * cap].astype(BF16)
+
+    for copy in swaps[: owners - 1]:
+        copy.wait_recv()
+    mine[0].wait()
+    repack(0)
+    for i in (2, 3, 4):
+        near[i].wait_recv()
+        own[i].wait()
+
+    def project(m, dst, first, last):
+        def step(s, carry):
+            dst[s] = dot(packed[0][...], weights[m][s], ROWS)
+            return carry
+
+        lax.fori_loop(first, last, step, 0)
+
+    project(0, pre_g, 0, 2)
+    project(1, pre_u, 0, 2)
+    forward(2)
+    for j in range(1, halves):
+        forwarded[2, j].wait_recv()
+    project(0, pre_g, 2, slots)
+    forward(3)
+    for j in range(1, halves):
+        forwarded[3, j].wait_recv()
+    project(1, pre_u, 2, slots)
+
+    def activate(s, carry):
+        _, silu = mix(pre_g[s], pre_u[s])
+        act[s] = (silu * pre_u[s]).astype(BF16)
+        return carry
+
+    lax.fori_loop(0, slots, activate, 0)
+    forward(4)
+    for j in range(1, halves):
+        forwarded[4, j].wait_recv()
+
+    def out_tile(at):
+        total = dot(act[0], weights[2][0, :, at])
+        for s in range(1, slots):
+            total = total + dot(act[s], weights[2][s, :, at])
+        put_rows(0, at, total)
+
+    tiles(out_tile)
+
+    for copy in swaps[owners - 1 :]:
+        copy.wait_recv()
+    mine[1].wait()
+    give_back(0)
+    repack(1)
+
+    def slope(s, carry):
+        d_act = dot(packed[1][...], weights[2][s], ROWS)
+        gate, up = pre_g[s], pre_u[s]
+        sigma, silu = mix(gate, up)
+        d_gate[s] = (d_act * up * (sigma * (1.0 + gate * (1.0 - sigma)))).astype(BF16)
+        d_up[s] = (d_act * silu).astype(BF16)
+        return carry
+
+    lax.fori_loop(0, slots, slope, 0)
+
+    def grad(s):
+        def body(at):
+            terms[0][s, :, at] = dot(d_gate[s], packed[0][:, at], COLS).astype(BF16)
+            terms[1][s, :, at] = dot(d_up[s], packed[0][:, at], COLS).astype(BF16)
+            terms[2][s, :, at] = dot(act[s], packed[1][:, at], COLS).astype(BF16)
+
+        tiles(body)
+
+    for j in range(1, halves):
+        grad(2 * j + 1)
+        for i in range(3):
+            reduce_near(i, j)
+        grad(2 * j)
+    for j in range(1, halves):
+        for i in range(5):
+            reduce_far(i, j)
+
+    def dx_tile(at):
+        total = dot(d_gate[0], weights[0][0, :, at]) + dot(d_up[0], weights[1][0, :, at])
+        for s in range(1, slots):
+            total = total + dot(d_gate[s], weights[0][s, :, at])
+            total = total + dot(d_up[s], weights[1][s, :, at])
+        put_rows(1, at, total)
+
+    for i in range(3):
+        for j in range(1, e_halves):
+            ex_near[i, j].wait_recv()
+            ex_held[i, j].wait()
+            add_rows(e_summed[i].at[j - 1], [e_arrived[i].at[j], e_held[i].at[j]])
+            other = lax.rem(e_half + j, e_halves) * 2 + e_side
+            ex_far[i, j] = go(
+                remote(
+                    e_summed[i].at[j - 1],
+                    e_landed[i].at[j - 1],
+                    ex_fs.at[i, j - 1],
+                    ex_fr.at[i, j - 1],
+                    "expert",
+                    other,
+                )
+            )
+    tiles(dx_tile)
+    grad(1)
+    for i in range(3):
+        reduce_near(i, 0)
+    give_back(1)
+    grad(0)
+
+    ends = list(sums) + list(hot_sums)
+    for i in (3, 4, 0, 1, 2):
+        rs_near[i, 0].wait_recv()
+        for j in range(1, halves):
+            rs_far[i, j].wait_recv()
+        add_rows(
+            ends[i],
+            [arrived[i].at[0], slot_of(locals_[i], 0)]
+            + [landed[i].at[j - 1] for j in range(1, halves)],
+        )
+    for i in range(3):
+        ex_near[i, 0].wait_recv()
+        ex_held[i, 0].wait()
+        for j in range(1, e_halves):
+            ex_far[i, j].wait_recv()
+        add_rows(
+            hot_grads[i],
+            [e_arrived[i].at[0], e_held[i].at[0]]
+            + [e_landed[i].at[j - 1] for j in range(1, e_halves)],
+        )
+    for group in (far, near, forwarded, rs_near, rs_far, ex_near, ex_far):
+        for copy in group.values():
+            copy.wait_send()
+    for copy in swaps:
+        copy.wait_send()
+    for copy in pending:
+        copy.wait()
+
+
+def layer(hot_in, cold_in, own_w, hot_w):
+    owners, halves = lax.axis_size("expert"), lax.axis_size("dp") // 2
+    e_halves, slots = owners // 2, 2 * halves
+    load, width = hot_in[0].shape
+    cap = cold_in[0].shape[1]
+    units = own_w[0].shape[0]
+    rows, part = owners * cap, width // owners
+    dma, vmem, shape = pltpu.SemaphoreType.DMA, pltpu.VMEM, jax.ShapeDtypeStruct
+    anywhere, inside = pl.BlockSpec(memory_space=pl.ANY), pl.BlockSpec(memory_space=pltpu.VMEM)
+    blocks = [(units, width)] * 3 + [(load, width)] * 2
+    scratch = [vmem((slots * load, width), BF16)] * 2 + [vmem((slots, units, width), BF16)] * 3
+    scratch += [vmem((owners, cap, width), BF16)] * 2 + [vmem((rows, width), BF16)] * 2
+    scratch += [vmem((slots, rows, units), F32)] * 2 + [vmem((slots, rows, units), BF16)] * 3
+    scratch += [vmem((owners, cap, width), BF16)] * 2 + [vmem((slots, units, width), BF16)] * 3
+    scratch += [vmem((slots * load, width), BF16)] * 2 + [vmem((units, width), BF16)] * 3
+    scratch += [vmem((halves,) + b, BF16) for b in blocks]
+    scratch += [vmem((halves - 1,) + b, BF16) for b in blocks] * 2
+    scratch += [vmem((e_halves, units, part), BF16)] * 6
+    scratch += [vmem((e_halves - 1, units, part), BF16)] * 6
+    scratch += [dma((9,)), dma((5, halves - 1)), dma((5, halves - 1)), dma((5,)), dma((5,))]
+    scratch += [dma((5, halves - 1))] * 2 + [dma((2, owners - 1))] * 4
+    scratch += [dma((5, halves))] * 2 + [dma((5, halves - 1))] * 2
+    scratch += [dma((3, e_halves))] * 2 + [dma((3, e_halves - 1))] * 2 + [dma((3, e_halves))]
+    outs = pl.pallas_call(
+        layer_kernel,
+        out_shape=[shape((owners, cap, width), BF16)] * 2
+        + [shape(b, BF16) for b in blocks]
+        + [shape((units, part), F32)] * 3,
+        in_specs=[anywhere] * 7 + [inside] * 3,
+        out_specs=[anywhere] * 2 + [inside] * 8,
+        scratch_shapes=scratch,
+        compiler_params=pltpu.CompilerParams(
+            collective_id=2, has_side_effects=True, vmem_limit_bytes=67043328
+        ),
+        name="layer",
+    )(*hot_in, *cold_in, *own_w, *hot_w)
+    return outs[2:], outs[:2]
+
+
 def local(
     tokens,
     cotangent,
@@ -354,46 +747,58 @@
     send_x = dot(either, tokens).astype(BF16)
     send_d = (gain * dot(either, cotangent)).astype(BF16)
 
-    (g_gate, g_up, g_down, hot_x, hot_d), (cold_x, cold_d) = dispatch(
-        (cold_gate[0], cold_up[0], cold_down[0], send_x[cold_total:], send_d[cold_total:]),
-        (
-            send_x[:cold_total].reshape(owners, capacity, width),
-            send_d[:cold_total].reshape(owners, capacity, width),
-        ),
-    )
-
-    hot_outs, hot_dxs, hot_grads = [], [], []
-    for h in range(hot_count):
-        rows_x = hot_x[:, h * hot_load : (h + 1) * hot_load].reshape(-1, width)
-        rows_d = hot_d[:, h * hot_load : (h + 1) * hot_load].reshape(-1, width)
-        out, dx, *grads = expert_block(rows_x, rows_d, hot_gate[h], hot_up[h], hot_down[h])
-        hot_outs.append(out.reshape(replicas, hot_load, width))
-        hot_dxs.append(dx.reshape(replicas, hot_load, width))
-        hot_grads.append(grads)
-    hot_out = jnp.concatenate(hot_outs, axis=1)
-    hot_dx = jnp.concatenate(hot_dxs, axis=1)
-    blocks = [
-        jnp.concatenate([grads[m] for grads in hot_grads], axis=0)
-        .reshape(hot_count * hot_units, owners, width // owners)
-        .transpose(1, 0, 2)
-        for m in range(3)
-    ]
-
-    out, dx, *terms = expert_block(
-        cold_x.reshape(cold_total, width),
-        cold_d.reshape(cold_total, width),
-        g_gate.reshape(-1, width),
-        g_up.reshape(-1, width),
-        g_down.reshape(-1, width),
-    )
-    units = cold_gate.shape[1]
-    terms = [term.reshape(replicas, units, width) for term in terms]
-    sums, (back_out, back_dx) = combine(
-        [("dp", term, BF16) for term in terms]
-        + [("dp", hot_out, BF16), ("dp", hot_dx, BF16)]
-        + [("expert", block, F32) for block in blocks],
-        (out.reshape(owners, capacity, width), dx.reshape(owners, capacity, width)),
-    )
+    fits = hot_count == 1 and owners <= 16 and width // owners % 128 == 0
+    if fits:
+        sums, (back_out, back_dx) = layer(
+            (send_x[cold_total:], send_d[cold_total:]),
+            (
+                send_x[:cold_total].reshape(owners, capacity, width),
+                send_d[:cold_total].reshape(owners, capacity, width),
+            ),
+            (cold_gate[0], cold_up[0], cold_down[0]),
+            (hot_gate[0], hot_up[0], hot_down[0]),
+        )
+    else:
+        (g_gate, g_up, g_down, hot_x, hot_d), (cold_x, cold_d) = dispatch(
+            (cold_gate[0], cold_up[0], cold_down[0], send_x[cold_total:], send_d[cold_total:]),
+            (
+                send_x[:cold_total].reshape(owners, capacity, width),
+                send_d[:cold_total].reshape(owners, capacity, width),
+            ),
+        )
+
+        hot_outs, hot_dxs, hot_grads = [], [], []
+        for h in range(hot_count):
+            rows_x = hot_x[:, h * hot_load : (h + 1) * hot_load].reshape(-1, width)
+            rows_d = hot_d[:, h * hot_load : (h + 1) * hot_load].reshape(-1, width)
+            out, dx, *grads = expert_block(rows_x, rows_d, hot_gate[h], hot_up[h], hot_down[h])
+            hot_outs.append(out.reshape(replicas, hot_load, width))
+            hot_dxs.append(dx.reshape(replicas, hot_load, width))
+            hot_grads.append(grads)
+        hot_out = jnp.concatenate(hot_outs, axis=1)
+        hot_dx = jnp.concatenate(hot_dxs, axis=1)
+        blocks = [
+            jnp.concatenate([grads[m] for grads in hot_grads], axis=0)
+            .reshape(hot_count * hot_units, owners, width // owners)
+            .transpose(1, 0, 2)
+            for m in range(3)
+        ]
+
+        out, dx, *terms = expert_block(
+            cold_x.reshape(cold_total, width),
+            cold_d.reshape(cold_total, width),
+            g_gate.reshape(-1, width),
+            g_up.reshape(-1, width),
+            g_down.reshape(-1, width),
+        )
+        units = cold_gate.shape[1]
+        terms = [term.reshape(replicas, units, width) for term in terms]
+        sums, (back_out, back_dx) = combine(
+            [("dp", term, BF16) for term in terms]
+            + [("dp", hot_out, BF16), ("dp", hot_dx, BF16)]
+            + [("expert", block, F32) for block in blocks],
+            (out.reshape(owners, capacity, width), dx.reshape(owners, capacity, width)),
+        )
     back_outs = jnp.concatenate([back_out.reshape(cold_total, width), sums[3]], axis=0)
     back_grads = jnp.concatenate([back_dx.reshape(cold_total, width), sums[4]], axis=0)
     outs = [dot(p, back_outs, COLS) for p in placing]

time: 200 us -> 174 us (0.87)
  matrix products: 32 us -> 6.91 us
  Pallas kernels: 150 us -> 153 us
    dot_general x15 -> x3, matrix products: 21.5 us -> 4.81 us  [dot(): return lax.dot_general(a, b, dims, preferred_element_type=F32)]
    dot_general x8 -> x2, matrix products: 10.4 us -> 2.1 us  [dot(): return jnp.dot(a, b, preferred_element_type=F32)]
    unnamed x38 -> x42, local copies, waits for them, and re-layouts: 8.31 us -> 5.26 us
    pallas_call x2 -> x1, Pallas kernels: 150 us -> 153 us  [layer(): pl.pallas_call(layer_kernel, out_shape=[shape((owners, cap, width), BF16)...]
where the time goes in v2:
time: 174 us
  Pallas kernels  153 us (88%)
  local copies, waits for them, and re-layouts  11.3 us (6%)
  matrix products  6.91 us (4%)
    pallas_call x1, Pallas kernels, layer(): pl.pallas_call(layer_kernel, out_shape=[shape((owners, cap, width), BF16)...  153 us
    unnamed x42, local copies, waits for them, and re-layouts  5.26 us
    dot_general x3, matrix products, dot(): return lax.dot_general(a, b, dims, preferred_element_type=F32)  4.81 us

profile of v2, /device:TPU:13, one launch (start us, length us, event | category | flops | bytes accessed | tf_op | source)
XLA Modules:
  0.0 174.0 jit_solution(11912851559001833355)
XLA Ops:
  0.6 0.8 slice_bitcast_fusion.3
  1.4 0.8 slice_bitcast_fusion.4
  2.2 0.8 slice_bitcast_fusion.2
  2.9 0.1 select_reduce_fusion.1
  3.0 0.8 fusion.22
  3.8 0.1 add_reduce_fusion
  4.0 0.0 copy-done.12
  4.0 0.0 copy-done.14
  4.0 1.6 fusion
  5.5 0.0 copy-start.3
  5.6 0.7 slice.45.refs_1_
  6.2 1.2 slice.47
  7.4 0.0 copy-done.8
  7.4 0.0 copy-done.10
  7.5 0.0 copy-done.3
  7.5 0.5 convolution_convert_fusion
  8.0 0.7 slice.44.refs_0_
  8.7 1.2 slice.46
  9.9 153.4 %layer.1 = (bf16[8,40,2048]{2,1,0:T(8,128)(2,1)}, bf16[8,40,2048]{2,1,0:T(8,128)(2,1)}, bf16[192,2048]{1,0:T(8,128)(2,1)}, bf16[192,2048]{1,0:T(8,128)(2,1)}, bf...) custom-call(bf16[32,2048]{1,0:T(8,128)(2,1)} %slice.44.refs_0_, ...), custom_call_target="tpu_custom_call" | custom-call | tf_op jit(solution)/shard_map/layer/pallas_call | solution.py:686
  163.3 0.0 copy-start.11
  163.3 0.0 copy-start.16
  163.3 0.0 copy-start.17
  163.3 2.8 %convolution_convert_fusion.1 = bf16[128,2048]{1,0:T(8,128)(2,1)} fusion(bf16[32,2048]{1,0:T(8,128)(2,1)} %get-tuple-element.22, bf16[320,2048]{1,0:T(8,128)(2,1)} %bitcast.71, s32[128]{0:T(128)} %copy-done.10, s32[128]{0:T(128)} %copy-done.8), kind=kOutput, calls=%fused_computation.3 | convolution fusion | flops 188055552 | bytes 1967104 | tf_op jit(solution)/shard_map/dot_general | solution.py:286
  166.1 0.0 copy-done.11
  166.1 0.0 copy-done.16
  166.1 0.0 copy-done.17
  166.2 0.0 copy-start.4
  166.2 0.0 copy-start.9
  166.2 0.0 copy-start.13
  166.2 0.0 copy-start.15
  166.2 0.5 fusion.6
  166.7 0.5 copy-done.4
  167.2 0.0 copy-done.9
  167.2 0.0 copy-done.13
  167.2 0.0 copy-done.15
  167.2 1.5 fusion.4
  168.7 0.6 pad_maximum_fusion.3
  169.3 0.0 copy-done.2
  169.3 0.9 copy.25
  170.2 0.0 copy-done.1
  170.2 0.9 copy.26
  171.1 0.0 copy-done
  171.1 0.9 copy.27
  172.0 0.0 copy-done.7
  172.0 0.7 copy.28
  172.6 0.0 copy-done.6
  172.6 0.7 copy.29
  173.3 0.7 copy.30
  (11 shorter events, 0.0 us)
Async XLA Ops:
  1.4 2.6 %copy-start.12 = (f32[128]{0:T(128)}, f32[128]{0:T(128)S(1)}, u32[]{:S(2)}) copy-start(f32[128]{0:T(128)S(1)} %get-tuple-element.34) | copy-start | bytes 1540
  1.4 2.6 %copy-start.14 = (f32[128]{0:T(128)}, f32[128]{0:T(128)S(1)}, u32[]{:S(2)}) copy-start(f32[128]{0:T(128)S(1)} %get-tuple-element.35) | copy-start | bytes 1540
  3.8 3.6 %copy-start.8 = (s32[128]{0:T(128)}, s32[128]{0:T(128)S(1)}, u32[]{:S(2)}) copy-start(s32[128]{0:T(128)S(1)} %get-tuple-element.36) | copy-start | bytes 1540
  3.8 3.6 %copy-start.10 = (s32[128]{0:T(128)}, s32[128]{0:T(128)S(1)}, u32[]{:S(2)}) copy-start(s32[128]{0:T(128)S(1)} %get-tuple-element.37) | copy-start | bytes 1540
  5.5 1.9 %copy-start.3 = (bf16[128,2048]{1,0:T(8,128)(2,1)S(1)}, bf16[128,2048]{1,0:T(8,128)(2,1)}, u32[]{:S(2)}) copy-start(bf16[128,2048]{1,0:T(8,128)(2,1)} %param.10) | copy-start | bytes 1572868
  163.3 2.8 %copy-start.11 = (s32[128]{0:T(128)S(1)}, s32[128]{0:T(128)}, u32[]{:S(2)}) copy-start(s32[128]{0:T(128)} %copy-done.10) | copy-start | bytes 1540
  163.3 2.8 %copy-start.16 = (bf16[8,40,2048]{2,1,0:T(8,128)(2,1)S(1)}, bf16[8,40,2048]{2,1,0:T(8,128)(2,1)}, u32[]{:S(2)}) copy-start(bf16[8,40,2048]{2,1,0:T(8,128)(2,1)} %get-tuple-element.19) | copy-start | bytes 3932164
  163.3 2.8 %copy-start.17 = (bf16[32,2048]{1,0:T(8,128)(2,1)S(1)}, bf16[32,2048]{1,0:T(8,128)(2,1)}, u32[]{:S(2)}) copy-start(bf16[32,2048]{1,0:T(8,128)(2,1)} %get-tuple-element.20) | copy-start | bytes 393220
  166.2 1.0 copy-start.4
  166.2 1.0 copy-start.9
  166.2 1.0 copy-start.13
  166.2 1.0 copy-start.15
  167.2 2.1 %copy-start.2 = (bf16[192,2048]{1,0:T(8,128)(2,1)S(1)}, bf16[192,2048]{1,0:T(8,128)(2,1)}, u32[]{:S(2)}) copy-start(bf16[192,2048]{1,0:T(8,128)(2,1)} %get-tuple-element.23) | copy-start | bytes 2359300
  168.7 1.5 copy-start.1
  169.3 1.8 %copy-start = (bf16[192,2048]{1,0:T(8,128)(2,1)S(1)}, bf16[192,2048]{1,0:T(8,128)(2,1)}, u32[]{:S(2)}) copy-start(bf16[192,2048]{1,0:T(8,128)(2,1)} %get-tuple-element.25) | copy-start | bytes 2359300
  170.2 1.8 %copy-start.7 = (f32[192,256]{1,0:T(8,128)S(1)}, f32[192,256]{1,0:T(8,128)}, u32[]{:S(2)}) copy-start(f32[192,256]{1,0:T(8,128)} %get-tuple-element.26) | copy-start | bytes 589828
  170.2 2.4 %copy-start.6 = (f32[192,256]{1,0:T(8,128)S(1)}, f32[192,256]{1,0:T(8,128)}, u32[]{:S(2)}) copy-start(f32[192,256]{1,0:T(8,128)} %get-tuple-element.27) | copy-start | bytes 589828
  171.1 2.2 %copy-start.5 = (f32[192,256]{1,0:T(8,128)S(1)}, f32[192,256]{1,0:T(8,128)}, u32[]{:S(2)}) copy-start(f32[192,256]{1,0:T(8,128)} %get-tuple-element.28) | copy-start | bytes 589828

commit v3 on v2

--- a/solution.py
+++ b/solution.py
@@ -312,7 +312,8 @@
 
 
 def layer_kernel(*refs):
-    hot_in, cold_in, own_w, hot_w = refs[:2], refs[2:4], refs[4:7], refs[7:10]
+    rows_in, own_w, hot_w = refs[:2], refs[2:5], refs[5:8]
+    refs = refs[:2] + refs
     back, sums, hot_sums, hot_grads = refs[10:12], refs[12:15], refs[15:17], refs[17:20]
     hot_rows, weights, landing, packed = refs[20:22], refs[22:25], refs[25:27], refs[27:29]
     pre_g, pre_u, act, d_gate, d_up = refs[29:34]
@@ -326,11 +327,15 @@
     owners = 2 * e_halves
     partner, e_partner = half * 2 + 1 - side, e_half * 2 + 1 - e_side
     slots = 2 * halves
-    load, width = hot_in[0].shape
-    cap = cold_in[0].shape[1]
+    cap, width = landing[0].shape[1:]
+    load = hot_rows[0].shape[0] // slots
+    hot_in = [ref.at[pl.ds(owners * cap, load)] for ref in rows_in]
     part = width // owners
     tile = 512 if width % 512 == 0 else width
     pending = []
+
+    def cold_in(i, index):
+        return rows_in[i].at[pl.ds(pl.multiple_of(index * cap, 8), cap)]
 
     def go(copy):
         copy.start()
@@ -393,7 +398,7 @@
             swaps.append(
                 go(
                     remote(
-                        cold_in[i].at[other],
+                        cold_in(i, other),
                         landing[i].at[rank],
                         sw_s.at[i, j - 1],
                         sw_r.at[i, j - 1],
@@ -405,7 +410,7 @@
         mine.append(
             go(
                 pltpu.make_async_copy(
-                    cold_in[i].at[rank], landing[i].at[rank], own_sem.at[5 + i]
+                    cold_in(i, rank), landing[i].at[rank], own_sem.at[5 + i]
                 )
             )
         )
@@ -470,9 +475,15 @@
     def columns(index):
         return pl.ds(pl.multiple_of(index * part, 128), part)
 
+    quads, quad, turn = e_halves // 2, e_half // 2, lax.rem(e_half, 2)
+
+    def facing(j):
+        other = turn if j % 2 == 0 else 1 - turn
+        return lax.rem(quad + j // 2, quads) * 2 + other
+
     for i in range(3):
         for j in list(range(1, e_halves)) + [0]:
-            to = lax.rem(e_half + j, e_halves) * 2
+            to = facing(j) * 2
             ex_near[i, j] = go(
                 remote(
                     hot_terms[i].at[:, columns(to + 1 - e_side)],
@@ -550,6 +561,26 @@
         forwarded[3, j].wait_recv()
     project(1, pre_u, 2, slots)
 
+    def cross(i, slot, index):
+        return go(
+            remote(
+                e_summed[i].at[slot],
+                e_landed[i].at[slot],
+                ex_fs.at[i, slot],
+                ex_fr.at[i, slot],
+                "expert",
+                index * 2 + e_side,
+            )
+        )
+
+    for i in range(3):
+        for k in list(range(1, quads)) + [0]:
+            j = 2 * k + 1
+            ex_near[i, j].wait_recv()
+            ex_held[i, j].wait()
+            add_rows(e_summed[i].at[k], [e_arrived[i].at[j], e_held[i].at[j]])
+            ex_far[i, k] = cross(i, k, quad * 2 + 1 - turn)
+
     def activate(s, carry):
         _, silu = mix(pre_g[s], pre_u[s])
         act[s] = (silu * pre_u[s]).astype(BF16)
@@ -583,6 +614,16 @@
         return carry
 
     lax.fori_loop(0, slots, slope, 0)
+    for i in range(3):
+        for k in range(1, quads):
+            slot, j = quads + k - 1, 2 * k
+            ex_near[i, j].wait_recv()
+            ex_held[i, j].wait()
+            ex_far[i, k].wait_recv()
+            add_rows(
+                e_summed[i].at[slot], [e_arrived[i].at[j], e_held[i].at[j], e_landed[i].at[k]]
+            )
+            ex_far[i, slot] = cross(i, slot, facing(j))
 
     def grad(s):
         def body(at):
@@ -608,22 +649,6 @@
             total = total + dot(d_up[s], weights[1][s, :, at])
         put_rows(1, at, total)
 
-    for i in range(3):
-        for j in range(1, e_halves):
-            ex_near[i, j].wait_recv()
-            ex_held[i, j].wait()
-            add_rows(e_summed[i].at[j - 1], [e_arrived[i].at[j], e_held[i].at[j]])
-            other = lax.rem(e_half + j, e_halves) * 2 + e_side
-            ex_far[i, j] = go(
-                remote(
-                    e_summed[i].at[j - 1],
-                    e_landed[i].at[j - 1],
-                    ex_fs.at[i, j - 1],
-                    ex_fr.at[i, j - 1],
-                    "expert",
-                    other,
-                )
-            )
     tiles(dx_tile)
     grad(1)
     for i in range(3):
@@ -644,12 +669,12 @@
     for i in range(3):
         ex_near[i, 0].wait_recv()
         ex_held[i, 0].wait()
-        for j in range(1, e_halves):
-            ex_far[i, j].wait_recv()
+        got = [slot for slot in range(e_halves - 1) if slot == 0 or slot >= quads]
+        for slot in got:
+            ex_far[i, slot].wait_recv()
         add_rows(
             hot_grads[i],
-            [e_arrived[i].at[0], e_held[i].at[0]]
-            + [e_landed[i].at[j - 1] for j in range(1, e_halves)],
+            [e_arrived[i].at[0], e_held[i].at[0]] + [e_landed[i].at[slot] for slot in got],
         )
     for group in (far, near, forwarded, rs_near, rs_far, ex_near, ex_far):
         for copy in group.values():
@@ -660,11 +685,10 @@
         copy.wait()
 
 
-def layer(hot_in, cold_in, own_w, hot_w):
+def layer(rows_in, cap, load, own_w, hot_w):
     owners, halves = lax.axis_size("expert"), lax.axis_size("dp") // 2
     e_halves, slots = owners // 2, 2 * halves
-    load, width = hot_in[0].shape
-    cap = cold_in[0].shape[1]
+    width = rows_in[0].shape[1]
     units = own_w[0].shape[0]
     rows, part = owners * cap, width // owners
     dma, vmem, shape = pltpu.SemaphoreType.DMA, pltpu.VMEM, jax.ShapeDtypeStruct
@@ -688,14 +712,14 @@
         out_shape=[shape((owners, cap, width), BF16)] * 2
         + [shape(b, BF16) for b in blocks]
         + [shape((units, part), F32)] * 3,
-        in_specs=[anywhere] * 7 + [inside] * 3,
+        in_specs=[anywhere] * 5 + [inside] * 3,
         out_specs=[anywhere] * 2 + [inside] * 8,
         scratch_shapes=scratch,
         compiler_params=pltpu.CompilerParams(
             collective_id=2, has_side_effects=True, vmem_limit_bytes=67043328
         ),
         name="layer",
-    )(*hot_in, *cold_in, *own_w, *hot_w)
+    )(*rows_in, *own_w, *hot_w)
     return outs[2:], outs[:2]
 
 
@@ -747,14 +771,12 @@
     send_x = dot(either, tokens).astype(BF16)
     send_d = (gain * dot(either, cotangent)).astype(BF16)
 
-    fits = hot_count == 1 and owners <= 16 and width // owners % 128 == 0
+    fits = hot_count == 1 and owners % 4 == 0 and owners <= 16 and width // owners % 128 == 0
     if fits:
         sums, (back_out, back_dx) = layer(
-            (send_x[cold_total:], send_d[cold_total:]),
-            (
-                send_x[:cold_total].reshape(owners, capacity, width),
-                send_d[:cold_total].reshape(owners, capacity, width),
-            ),
+            (send_x, send_d),
+            capacity,
+            hot_load,
             (cold_gate[0], cold_up[0], cold_down[0]),
             (hot_gate[0], hot_up[0], hot_down[0]),
         )

time: 174 us -> 170 us (0.977)
  the two profiles are of different devices: /device:TPU:13 before, /device:TPU:4 now
where the time goes in v3:
time: 170 us
  Pallas kernels  151 us (89%)
  matrix products  9.14 us (5%)
  local copies, waits for them, and re-layouts  7.52 us (4%)
    pallas_call x1, Pallas kernels, layer(): pl.pallas_call(layer_kernel, out_shape=[shape((owners, cap, width), BF16)...  151 us
    unnamed x42, local copies, waits for them, and re-layouts  5.25 us
    dot_general x3, matrix products, dot(): return lax.dot_general(a, b, dims, preferred_element_type=F32)  4.81 us
    dot_general x2, matrix products, dot(): return jnp.dot(a, b, preferred_element_type=F32)  4.33 us

profile of v3, /device:TPU:4, one launch (start us, length us, event | category | flops | bytes accessed | tf_op | source)
XLA Modules:
  0.0 169.6 jit_solution(976187374483431584)
XLA Ops:
  0.6 0.0 copy-start.3
  0.7 0.8 slice_bitcast_fusion.3
  1.4 0.0 copy-start.14
  1.4 0.8 slice_bitcast_fusion.4
  2.2 0.8 slice_bitcast_fusion.2
  2.9 0.1 select_reduce_fusion.1
  3.0 0.8 fusion.22
  3.8 0.0 copy-start.8
  3.8 0.0 copy-start.10
  3.8 0.0 copy-done.12
  3.8 0.0 copy-done.14
  3.8 0.1 add_reduce_fusion
  4.0 2.7 %fusion.refs_1_ = bf16[352,2048]{1,0:T(8,128)(2,1)} fusion(bf16[128,2048]{1,0:T(8,128)(2,1)} %param.11, f32[352]{0:T(512)S(1)} %add_reduce_fusion, s32[128]{0:T(128)S(1)} %get-tuple-element.37, s32[128]{0:T(128)S(1)} %get-tuple-element.36), kind=kOutput, calls=%fused_computation.1 | convolution fusion | flops 186351616 | bytes 1968512 | tf_op jit(solution)/shard_map/dot_general | solution.py:285
  6.7 0.0 copy-done.8
  6.7 0.0 copy-done.10
  6.7 0.0 copy-done.3
  6.7 1.7 convolution_convert_fusion.refs_0_
  8.3 150.6 %layer.1 = (bf16[8,40,2048]{2,1,0:T(8,128)(2,1)}, bf16[8,40,2048]{2,1,0:T(8,128)(2,1)}, bf16[192,2048]{1,0:T(8,128)(2,1)}, bf16[192,2048]{1,0:T(8,128)(2,1)}, bf...) custom-call(bf16[352,2048]{1,0:T(8,128)(2,1)} %convolution_convert_f, ...), custom_call_target="tpu_custom_call" | custom-call | tf_op jit(solution)/shard_map/layer/pallas_call | solution.py:710
  158.9 0.0 copy-start.11
  158.9 0.0 copy-start.16
  159.0 0.0 copy-start.17
  159.0 2.8 %convolution_convert_fusion.1 = bf16[128,2048]{1,0:T(8,128)(2,1)} fusion(bf16[32,2048]{1,0:T(8,128)(2,1)} %get-tuple-element.22, bf16[320,2048]{1,0:T(8,128)(2,1)} %bitcast.67, s32[128]{0:T(128)} %copy-done.10, s32[128]{0:T(128)} %copy-done.8), kind=kOutput, calls=%fused_computation.3 | convolution fusion | flops 188055552 | bytes 1967104 | tf_op jit(solution)/shard_map/dot_general | solution.py:286
  161.8 0.0 copy-done.11
  161.8 0.0 copy-done.16
  161.8 0.0 copy-done.17
  161.8 0.0 copy-start.4
  161.8 0.0 copy-start.9
  161.8 0.0 copy-start.13
  161.8 0.0 copy-start.15
  161.8 0.5 fusion.6
  162.3 0.5 copy-done.4
  162.8 0.0 copy-done.9
  162.8 0.0 copy-done.13
  162.8 0.0 copy-done.15
  162.8 1.5 fusion.4
  164.4 0.6 pad_maximum_fusion.3
  164.9 0.0 copy-done.2
  164.9 0.9 copy.25
  165.8 0.0 copy-done.1
  165.8 0.9 copy.26
  166.7 0.0 copy-done
  166.7 0.9 copy.27
  167.6 0.0 copy-done.7
  167.6 0.7 copy.28
  168.3 0.0 copy-done.6
  168.3 0.7 copy.29
  168.9 0.0 copy-done.5
  169.0 0.7 copy.30
  (7 shorter events, 0.0 us)
Async XLA Ops:
  0.6 6.0 %copy-start.3 = (bf16[128,2048]{1,0:T(8,128)(2,1)S(1)}, bf16[128,2048]{1,0:T(8,128)(2,1)}, u32[]{:S(2)}) copy-start(bf16[128,2048]{1,0:T(8,128)(2,1)} %param.10) | copy-start | bytes 1572868
  1.4 2.4 %copy-start.12 = (f32[128]{0:T(128)}, f32[128]{0:T(128)S(1)}, u32[]{:S(2)}) copy-start(f32[128]{0:T(128)S(1)} %get-tuple-element.34) | copy-start | bytes 1540
  1.4 2.4 %copy-start.14 = (f32[128]{0:T(128)}, f32[128]{0:T(128)S(1)}, u32[]{:S(2)}) copy-start(f32[128]{0:T(128)S(1)} %get-tuple-element.35) | copy-start | bytes 1540
  3.8 2.8 %copy-start.8 = (s32[128]{0:T(128)}, s32[128]{0:T(128)S(1)}, u32[]{:S(2)}) copy-start(s32[128]{0:T(128)S(1)} %get-tuple-element.36) | copy-start | bytes 1540
  3.8 2.8 %copy-start.10 = (s32[128]{0:T(128)}, s32[128]{0:T(128)S(1)}, u32[]{:S(2)}) copy-start(s32[128]{0:T(128)S(1)} %get-tuple-element.37) | copy-start | bytes 1540
  158.9 2.8 %copy-start.11 = (s32[128]{0:T(128)S(1)}, s32[128]{0:T(128)}, u32[]{:S(2)}) copy-start(s32[128]{0:T(128)} %copy-done.10) | copy-start | bytes 1540
  158.9 2.8 %copy-start.16 = (bf16[8,40,2048]{2,1,0:T(8,128)(2,1)S(1)}, bf16[8,40,2048]{2,1,0:T(8,128)(2,1)}, u32[]{:S(2)}) copy-start(bf16[8,40,2048]{2,1,0:T(8,128)(2,1)} %get-tuple-element.19) | copy-start | bytes 3932164
  159.0 2.8 %copy-start.17 = (bf16[32,2048]{1,0:T(8,128)(2,1)S(1)}, bf16[32,2048]{1,0:T(8,128)(2,1)}, u32[]{:S(2)}) copy-start(bf16[32,2048]{1,0:T(8,128)(2,1)} %get-tuple-element.20) | copy-start | bytes 393220
  161.8 1.0 copy-start.4
  161.8 1.0 copy-start.9
  161.8 1.0 copy-start.13
  161.8 1.0 copy-start.15
  162.8 2.1 %copy-start.2 = (bf16[192,2048]{1,0:T(8,128)(2,1)S(1)}, bf16[192,2048]{1,0:T(8,128)(2,1)}, u32[]{:S(2)}) copy-start(bf16[192,2048]{1,0:T(8,128)(2,1)} %get-tuple-element.23) | copy-start | bytes 2359300
  164.4 1.5 copy-start.1
  164.9 1.8 %copy-start = (bf16[192,2048]{1,0:T(8,128)(2,1)S(1)}, bf16[192,2048]{1,0:T(8,128)(2,1)}, u32[]{:S(2)}) copy-start(bf16[192,2048]{1,0:T(8,128)(2,1)} %get-tuple-element.25) | copy-start | bytes 2359300
  165.8 1.8 %copy-start.7 = (f32[192,256]{1,0:T(8,128)S(1)}, f32[192,256]{1,0:T(8,128)}, u32[]{:S(2)}) copy-start(f32[192,256]{1,0:T(8,128)} %get-tuple-element.26) | copy-start | bytes 589828
  165.8 2.4 %copy-start.6 = (f32[192,256]{1,0:T(8,128)S(1)}, f32[192,256]{1,0:T(8,128)}, u32[]{:S(2)}) copy-start(f32[192,256]{1,0:T(8,128)} %get-tuple-element.27) | copy-start | bytes 589828
  166.7 2.2 %copy-start.5 = (f32[192,256]{1,0:T(8,128)S(1)}, f32[192,256]{1,0:T(8,128)}, u32[]{:S(2)}) copy-start(f32[192,256]{1,0:T(8,128)} %get-tuple-element.28) | copy-start | bytes 589828
